TPU v7x, 512 devices: a whole 4x8x8 slice. The times are simulated.
512 devices in a mesh: row: 32 (over y, z_hi, core), col: 16 (over x, z_lo).
Axes of the slice: x: 4, y: 8, z: 8 (z_hi: 2, z_lo: 4; z = z_hi * 4 + z_lo), core: 2. Of those that a mesh axis runs over, the one named last changes fastest.
Arguments:
- features: bfloat16 [32, 16, 128, 128], P('row', 'col'), may hold values from -6 to 6
- tiles: bfloat16 [32, 16, 128, 128, 128], P('row', 'col'), may hold values from -0.3984375 to 0.3984375
- tile_coords: int32 [32, 16, 128, 2], P('row', 'col'), may hold values from 0 to 31, as said below
- tile_count: int32 [32, 16], P('row', 'col'), may hold values from 1 to 128, as said below
- batch_mask: int32 [32, 16, 128], P('row', 'col'), may hold values 0 or 1
- history: bfloat16 [32, 16, 128, 256], P('row', 'col'), may hold values from 0 to 1.5
- weight_one: bfloat16 [128, 256], replicated, may hold values from -0.5 to 0.5
- bias_one: float32 [256], replicated, may hold values from -3 to 3
- weight_two: bfloat16 [256, 172], replicated, may hold values from -0.375 to 0.375
- bias_two: float32 [172], replicated, may hold values from -3 to 3
Outputs:
- new_history: bfloat16 [32, 16, 128, 256], P('row', 'col')
- logits: float32 [32, 16, 128, 172], P('row', 'col')
Inputs may be any that keep to these rules, and one draw needn't show every extreme that they name: `tile_coords`: column 0 is below 16 and column 1 below 32; coordinates may repeat. `tile_count`: some device has all 128 slots live.
All inputs are finite; a program needn't handle non-finite values. No bound on the sum of `batch_mask` on one device may be relied on, other than what follows from the above.
Results may differ from a plain program's by a relative error of at most 0.024.
Values may be sent and summed in bfloat16 or wider, within the bound.
A program may use at most 64 MiB of HBM per device.

v0:
```python
import jax
import jax.numpy as jnp
from jax import lax
from jax.sharding import PartitionSpec as P


def joined_along(tiles, dim):
    tiles = jnp.moveaxis(tiles, 0, dim)
    lengths = tiles.shape
    return tiles.reshape(*lengths[:dim], lengths[dim] * lengths[dim + 1], *lengths[dim + 2 :])


def copy_for_each(shard, axis):
    copies = jnp.broadcast_to(shard, (lax.axis_size(axis), *shard.shape))
    return lax.all_to_all(copies, axis, split_axis=0, concat_axis=0, tiled=True)


def collect(shard, axis, dim):
    return joined_along(copy_for_each(shard, axis), dim)


def in_blocks(shard, dim, size):
    lengths = shard.shape
    tiles = shard.reshape(*lengths[:dim], size, lengths[dim] // size, *lengths[dim + 1 :])
    return jnp.moveaxis(tiles, dim, 0)


def sent_and_summed(shard, axis, dim):
    tiles = in_blocks(shard, dim, lax.axis_size(axis))
    arrived = lax.all_to_all(tiles, axis, split_axis=0, concat_axis=0, tiled=True)
    return arrived.astype(jnp.float32).sum(axis=0)


def tile_products(gathered, tiles, coords, live_total, group_size, group_count):
    row_blocks = lax.axis_size("col")
    block_ids = jnp.arange(row_blocks, dtype=jnp.int32)

    def one_group(step, running):
        first = step * group_size
        tile_group = lax.dynamic_slice_in_dim(tiles, first, group_size, 0)
        coord_group = lax.dynamic_slice_in_dim(coords, first, group_size, 0)
        sources = jnp.take(gathered, coord_group[:, 1], axis=0)
        products = jnp.einsum(
            "gij,gjf->gif", tile_group, sources, preferred_element_type=jnp.float32
        )
        slot_ids = first + jnp.arange(group_size, dtype=jnp.int32)
        alive = (slot_ids < live_total).astype(jnp.float32)
        placing = (coord_group[:, 0][None, :] == block_ids[:, None]).astype(jnp.float32) * alive[
            None, :
        ]
        return running + jnp.einsum(
            "rg,gif->rif", placing, products, precision=lax.Precision.HIGHEST
        )

    start_total = jnp.zeros((row_blocks, gathered.shape[1], gathered.shape[2]), jnp.float32)
    return lax.fori_loop(0, group_count, one_group, start_total)


def on_device(
    features,
    tiles,
    tile_coords,
    tile_count,
    batch_mask,
    history,
    weight_one,
    bias_one,
    weight_two,
    bias_two,
):
    tile_set = tiles[0, 0]
    coord_set = tile_coords[0, 0]
    live_total = tile_count[0, 0]
    slots = tile_set.shape[0]
    group_size = 16
    group_count = (live_total + group_size - 1) // group_size
    gathered_input = collect(features[0], "row", 0)
    summed_one = tile_products(
        gathered_input, tile_set, coord_set, live_total, group_size, group_count
    )
    owned_one = sent_and_summed(summed_one.astype(jnp.bfloat16), "col", 0)[0]
    agg_one = (features[0, 0].astype(jnp.float32) + owned_one).astype(jnp.bfloat16)
    pre_one = jnp.dot(agg_one, weight_one, preferred_element_type=jnp.float32) + bias_one
    hidden = jax.nn.relu(pre_one).astype(jnp.bfloat16)
    pushed = jnp.where(batch_mask[0, 0][:, None] == 1, hidden, history[0, 0])
    projected = jnp.dot(pushed, weight_two, preferred_element_type=jnp.float32).astype(jnp.bfloat16)
    gathered_proj = collect(projected[None], "row", 0)
    summed_two = tile_products(
        gathered_proj, tile_set, coord_set, live_total, group_size, group_count
    )
    owned_two = sent_and_summed(summed_two.astype(jnp.bfloat16), "col", 0)[0]
    scores = projected.astype(jnp.float32) + owned_two + bias_two
    return (pushed[None, None], scores[None, None])


def solution(mesh):
    return jax.shard_map(
        on_device,
        mesh=mesh,
        in_specs=(
            P("row", "col", None, None),
            P("row", "col", None, None, None),
            P("row", "col", None, None),
            P("row", "col"),
            P("row", "col", None),
            P("row", "col", None, None),
            P(),
            P(),
            P(),
            P(),
        ),
        out_specs=(P("row", "col", None, None), P("row", "col", None, None)),
        check_vma=False,
    )
```

profile of v0, /device:TPU:8, one launch (start us, length us, event | category | flops | bytes accessed | tf_op | source)
XLA Modules:
  0.0 234.8 jit_solution(13238899792525449773)
XLA Ops:
  0.6 2.0 broadcast_in_dim.55
  2.6 16.3 %all-to-all-start = ((bf16[32,1,128,128]{3,2,1,0:T(8,128)(2,1)}), bf16[32,1,128,128]{3,2,1,0:T(8,128)(2,1)S(1)}, u32[]{:S(2)}, u32[]{:S(2)}) async-start(bf16[32,1,128,128]{3,2,1,0:T(8,128)(2,1)} %broadcast_in_dim.55), calls=%async_computation | async-start | bytes 2097152 | tf_op jit(solution)/shard_map/all_to_all | solution.py:15
  19.6 30.0 %all-to-all-done = bf16[32,1,128,128]{3,2,1,0:T(8,128)(2,1)S(1)} async-done(((bf16[32,1,128,128]{3,2,1,0:T(8,128)(2,1)}), bf16[32,1,128,128]{3,2,1,0:T(8,128)(2,1)S(1)}, u32[]{:S(2)}, u32[]{:S(2)}) %all-to-all-start) | async-done | bytes 1048608 | tf_op jit(solution)/shard_map/all_to_all | solution.py:15
  49.7 23.2 %while.22 = (s32[]{:T(128)}, f32[16,128,128]{2,0,1:T(8,128)S(1)}, s32[]{:T(128)}, s32[128,2]{0,1:T(2,128)S(1)}, s32[]{:T(128)}, /*index=5*/bf16[128,128,128]{2,1...) while((s32[]{:T(128)}, f32[16,128,128]{2,0,1:T(8,128)S(1)}, ...), condition=%wide.region_1.2_spmd.clone, body=%wide.region_0.1_spmd.clone.sunk | while | flops 117966536 | bytes 6296651 | solution.py:56
  52.6 1.8 convolution_add_fusion.5
  57.2 1.8 convolution_add_fusion.5
  61.8 1.8 convolution_add_fusion.5
  74.1 18.7 %all-to-all-start.1 = ((bf16[16,1,128,128]{3,2,1,0:T(8,128)(2,1)}), bf16[16,1,128,128]{3,2,1,0:T(8,128)(2,1)S(1)}, u32[]{:S(2)}, u32[]{:S(2)}) async-start(bf16[16,1,128,128]{3,2,1,0:T(8,128)(2,1)} %bitcast.43), calls=%async_computation.1 | async-start | bytes 1048576 | tf_op jit(solution)/shard_map/all_to_all | solution.py:30
  92.8 15.0 %all-to-all-done.1 = bf16[16,1,128,128]{3,2,1,0:T(8,128)(2,1)S(1)} async-done(((bf16[16,1,128,128]{3,2,1,0:T(8,128)(2,1)}), bf16[16,1,128,128]{3,2,1,0:T(8,128)(2,1)S(1)}, u32[]{:S(2)}, u32[]{:S(2)}) %all-to-all-start.1) | async-done | bytes 524320 | tf_op jit(solution)/shard_map/all_to_all | solution.py:30
  109.6 8.2 %all-to-all-start.2 = ((bf16[32,1,128,172]{2,3,1,0:T(8,128)(2,1)}), bf16[32,1,128,172]{2,3,1,0:T(8,128)(2,1)S(1)}, u32[]{:S(2)}, u32[]{:S(2)}) async-start(bf16[32,1,128,172]{2,3,1,0:T(8,128)(2,1)} %broadcast_in_dim.58), calls=%async_computation.2 | async-start | bytes 2883584 | tf_op jit(solution)/shard_map/all_to_all | solution.py:15
  117.7 38.7 %all-to-all-done.2 = bf16[32,1,128,172]{2,3,1,0:T(8,128)(2,1)S(1)} async-done(((bf16[32,1,128,172]{2,3,1,0:T(8,128)(2,1)}), bf16[32,1,128,172]{2,3,1,0:T(8,128)(2,1)S(1)}, u32[]{:S(2)}, u32[]{:S(2)}) %all-to-all-start.2) | async-done | bytes 1409056 | tf_op jit(solution)/shard_map/all_to_all | solution.py:15
  156.5 3.0 %copy.15 = bf16[32,128,172]{2,1,0:T(8,128)(2,1)} copy(bf16[32,128,172]{1,2,0:T(8,128)(2,1)S(1)} %bitcast.59) | data formatting | bytes 2818048
  159.5 32.9 %while.23 = (s32[]{:T(128)}, f32[16,128,172]{1,0,2:T(8,128)S(1)}, s32[]{:T(128)}, s32[128,2]{0,1:T(2,128)S(1)}, s32[]{:T(128)}, /*index=5*/bf16[128,128,128]{2,1...) while((s32[]{:T(128)}, f32[16,128,172]{1,0,2:T(8,128)S(1)}, ...), condition=%wide.region_4.5_spmd.clone, body=%wide.region_3.4_spmd.clone.sunk | while | flops 158516928 | bytes 8279115 | solution.py:56
  160.3 2.2 gather_fusion.1
  164.2 2.0 convolution_add_fusion.6
  166.9 2.2 gather_fusion.1
  170.7 2.0 convolution_add_fusion.6
  173.5 2.2 gather_fusion.1
  177.3 2.0 convolution_add_fusion.6
  180.1 2.2 gather_fusion.1
  183.9 2.0 convolution_add_fusion.6
  186.6 2.2 gather_fusion.1
  190.4 2.0 convolution_add_fusion.6
  192.9 41.0 %all_to_all.20 = bf16[16,1,128,172]{2,3,1,0:T(8,128)(2,1)S(1)} all-to-all(bf16[16,1,128,172]{2,3,1,0:T(8,128)(2,1)S(1)} %bitcast.60), channel_id=1, replica_groups=mesh['row'=32,'col'=16] {'col'}, dimensions={0} | all-to-all | bytes 1409024 | tf_op jit(solution)/shard_map/all_to_all | solution.py:30
  (97 shorter events, 33.8 us)
Async XLA Ops:
  0.6 107.4 %copy-start = (bf16[256,172]{0,1:T(8,128)(2,1)S(1)}, bf16[256,172]{0,1:T(8,128)(2,1)}, u32[]{:S(2)}) copy-start(bf16[256,172]{0,1:T(8,128)(2,1)} %param.22) | copy-start | bytes 264196
  2.6 47.0 %copy-start.3 = (s32[1,1,128,2]{2,3,1,0:T(2,128)S(1)}, s32[1,1,128,2]{2,3,1,0:T(2,128)}, u32[]{:S(2)}) copy-start(s32[1,1,128,2]{2,3,1,0:T(2,128)} %param.16) | copy-start | bytes 3076
  2.6 47.0 %all-to-all-start = ((bf16[32,1,128,128]{3,2,1,0:T(8,128)(2,1)}), bf16[32,1,128,128]{3,2,1,0:T(8,128)(2,1)S(1)}, u32[]{:S(2)}, u32[]{:S(2)}) async-start(bf16[32,1,128,128]{3,2,1,0:T(8,128)(2,1)} %broadcast_in_dim.55), calls=%async_computation | async-start | bytes 2097152 | tf_op jit(solution)/shard_map/all_to_all | solution.py:15
  72.9 19.9 %copy-start.8 = (s32[1,1,128]{2,1,0:T(1,128)S(1)}, s32[1,1,128]{2,1,0:T(1,128)}, u32[]{:S(2)}) copy-start(s32[1,1,128]{2,1,0:T(1,128)} %param.18) | copy-start | bytes 1540
  72.9 34.9 %copy-start.2 = (bf16[1,1,128,128]{3,2,1,0:T(8,128)(2,1)S(1)}, bf16[1,1,128,128]{3,2,1,0:T(8,128)(2,1)}, u32[]{:S(2)}) copy-start(bf16[1,1,128,128]{3,2,1,0:T(8,128)(2,1)} %param.14) | copy-start | bytes 98308
  73.0 34.9 %copy-start.4 = (bf16[128,256]{1,0:T(8,128)(2,1)S(1)}, bf16[128,256]{1,0:T(8,128)(2,1)}, u32[]{:S(2)}) copy-start(bf16[128,256]{1,0:T(8,128)(2,1)} %param.20) | copy-start | bytes 196612
  73.0 34.9 %copy-start.5 = (bf16[1,1,128,256]{3,2,1,0:T(8,128)(2,1)S(1)}, bf16[1,1,128,256]{3,2,1,0:T(8,128)(2,1)}, u32[]{:S(2)}) copy-start(bf16[1,1,128,256]{3,2,1,0:T(8,128)(2,1)} %param.19) | copy-start | bytes 196612
  73.0 34.9 %copy-start.6 = (f32[256]{0:T(256)S(1)}, f32[256]{0:T(256)}, u32[]{:S(2)}) copy-start(f32[256]{0:T(256)} %param.21) | copy-start | bytes 3076
  74.1 33.6 %all-to-all-start.1 = ((bf16[16,1,128,128]{3,2,1,0:T(8,128)(2,1)}), bf16[16,1,128,128]{3,2,1,0:T(8,128)(2,1)S(1)}, u32[]{:S(2)}, u32[]{:S(2)}) async-start(bf16[16,1,128,128]{3,2,1,0:T(8,128)(2,1)} %bitcast.43), calls=%async_computation.1 | async-start | bytes 1048576 | tf_op jit(solution)/shard_map/all_to_all | solution.py:30
  108.1 1.5 copy-start.1
  109.6 46.9 %all-to-all-start.2 = ((bf16[32,1,128,172]{2,3,1,0:T(8,128)(2,1)}), bf16[32,1,128,172]{2,3,1,0:T(8,128)(2,1)S(1)}, u32[]{:S(2)}, u32[]{:S(2)}) async-start(bf16[32,1,128,172]{2,3,1,0:T(8,128)(2,1)} %broadcast_in_dim.58), calls=%async_computation.2 | async-start | bytes 2883584 | tf_op jit(solution)/shard_map/all_to_all | solution.py:15
  192.9 41.1 %copy-start.7 = (f32[172]{0:T(256)S(1)}, f32[172]{0:T(256)}, u32[]{:S(2)}) copy-start(f32[172]{0:T(256)} %param.23) | copy-start | bytes 2068
where the time goes:
time: 236 us; the launch traced here: 235 us
  waiting for transfers between devices  83.7 us (35%)
  starting transfers between devices  43.1 us (18%)
  blocking collectives  41 us (17%)
  matrix products  34.1 us (14%)
  local copies, waits for them, and re-layouts  23.9 us (10%)
  other arithmetic  7.04 us (3%)
    all_to_all x2, waiting for transfers between devices, copy_for_each(): return lax.all_to_all(copies, axis, split_axis=0, concat_axis=0, tiled=True)  68.7 us
    all_to_all x1, blocking collectives, sent_and_summed(): lax.all_to_all(tiles, axis, split_axis=0, concat_axis=0, tiled=True)  41 us
    all_to_all x2, starting transfers between devices, copy_for_each(): return lax.all_to_all(copies, axis, split_axis=0, concat_axis=0, tiled=True)  24.5 us
    dot_general x10, matrix products, one_group(): jnp.einsum('rg,gif->rif', placing, products, precision=lax.Precision.HIGH...  18.7 us
    all_to_all x1, starting transfers between devices, sent_and_summed(): lax.all_to_all(tiles, axis, split_axis=0, concat_axis=0, tiled=True)  18.7 us
    dot_general x10, matrix products, one_group(): jnp.einsum('gij,gjf->gif', tile_group, sources, preferred_element_type=jn...  15.1 us
    all_to_all x1, waiting for transfers between devices, sent_and_summed(): lax.all_to_all(tiles, axis, split_axis=0, concat_axis=0, tiled=True)  15 us
    gather x10, local copies, waits for them, and re-layouts, one_group(): sources = jnp.take(gathered, coord_group[:, 1], axis=0)  14.3 us
  transfers between devices with their start and end apart: 3, of which 3 were waited for; matrix products, arithmetic and copies ran while one was open for 0% of the time, Pallas kernels for 0%

commit v1 on v0

--- a/solution.py
+++ b/solution.py
@@ -74,21 +74,25 @@
     slots = tile_set.shape[0]
     group_size = 16
     group_count = (live_total + group_size - 1) // group_size
-    gathered_input = collect(features[0], "row", 0)
+    gathered_input = lax.all_gather(features[0, 0], "row", axis=0)
     summed_one = tile_products(
         gathered_input, tile_set, coord_set, live_total, group_size, group_count
     )
-    owned_one = sent_and_summed(summed_one.astype(jnp.bfloat16), "col", 0)[0]
+    owned_one = lax.psum_scatter(
+        summed_one.astype(jnp.bfloat16).astype(jnp.float32), "col", scatter_dimension=0
+    )
     agg_one = (features[0, 0].astype(jnp.float32) + owned_one).astype(jnp.bfloat16)
     pre_one = jnp.dot(agg_one, weight_one, preferred_element_type=jnp.float32) + bias_one
     hidden = jax.nn.relu(pre_one).astype(jnp.bfloat16)
     pushed = jnp.where(batch_mask[0, 0][:, None] == 1, hidden, history[0, 0])
     projected = jnp.dot(pushed, weight_two, preferred_element_type=jnp.float32).astype(jnp.bfloat16)
-    gathered_proj = collect(projected[None], "row", 0)
+    gathered_proj = lax.all_gather(projected, "row", axis=0)
     summed_two = tile_products(
         gathered_proj, tile_set, coord_set, live_total, group_size, group_count
     )
-    owned_two = sent_and_summed(summed_two.astype(jnp.bfloat16), "col", 0)[0]
+    owned_two = lax.psum_scatter(
+        summed_two.astype(jnp.bfloat16).astype(jnp.float32), "col", scatter_dimension=0
+    )
     scores = projected.astype(jnp.float32) + owned_two + bias_two
     return (pushed[None, None], scores[None, None])
 

time: 236 us -> 567 us (2.40)
  the two profiles are of different devices: /device:TPU:8 before, /device:TPU:1 now
where the time goes in v1:
time: 567 us; the launch traced here: 557 us
  waiting for transfers between devices  477 us (84%)
  matrix products  28.8 us (5%)
  local copies, waits for them, and re-layouts  28 us (5%)
  between operations  14.6 us (3%)
  other arithmetic  8.03 us (1%)
    unnamed x5, waiting for transfers between devices  184 us
    all_gather x1, waiting for transfers between devices, on_device(): gathered_proj = lax.all_gather(projected, 'row', axis=0)  98.8 us
    all_gather x1, waiting for transfers between devices, on_device(): gathered_input = lax.all_gather(features[0, 0], 'row', axis=0)  97.3 us
    reduce_scatter x1, waiting for transfers between devices, on_device(): lax.psum_scatter(summed_one.astype(jnp.bfloat16).astype(jnp.float32), 'co...  96.9 us
    gather x8, local copies, waits for them, and re-layouts, one_group(): sources = jnp.take(gathered, coord_group[:, 1], axis=0)  16.3 us
    dot_general x8, matrix products, one_group(): jnp.einsum('rg,gif->rif', placing, products, precision=lax.Precision.HIGH...  14.9 us
    dot_general x8, matrix products, one_group(): jnp.einsum('gij,gjf->gif', tile_group, sources, preferred_element_type=jn...  12 us
  transfers between devices with their start and end apart: 4, of which 4 were waited for; matrix products, arithmetic and copies ran while one was open for 0% of the time, Pallas kernels for 0%

profile of v1, /device:TPU:1, one launch (start us, length us, event | category | flops | bytes accessed | tf_op | source)
XLA Modules:
  0.0 556.5 jit_solution(12759802306007417757)
XLA Ops:
  8.6 97.3 %all-gather.5.cloned.1.call-done = bf16[32,1,128,128]{3,2,1,0:T(8,128)(2,1)} async-done(((bf16[1,1,128,128]{3,2,1,0:T(8,128)(2,1)}), bf16[32,1,128,128]{3,2,1,0:T(8,128)(2,1)}) %all-gather.5.cloned.1.call-update) | async-done | bytes 1048592 | tf_op jit(solution)/shard_map/all_gather | solution.py:77
  106.0 26.2 %while.22 = (s32[]{:T(128)}, f32[16,128,128]{2,0,1:T(8,128)S(1)}, s32[]{:T(128)}, s32[128,2]{0,1:T(2,128)}, s32[]{:T(128)}, /*index=5*/bf16[128,128,128]{2,1,0:T...) while((s32[]{:T(128)}, f32[16,128,128]{2,0,1:T(8,128)S(1)}, ...), condition=%wide.region_1.2_spmd.clone, body=%wide.region_0.1_spmd.clone.sunk | while | flops 117966536 | bytes 6296651 | solution.py:56
  106.8 1.9 gather_fusion
  110.8 1.8 convolution_add_fusion.5
  113.3 1.9 gather_fusion
  117.3 1.8 convolution_add_fusion.5
  119.9 1.9 gather_fusion
  123.9 1.8 convolution_add_fusion.5
  126.4 1.9 gather_fusion
  130.4 1.8 convolution_add_fusion.5
  133.7 96.9 %reduce-scatter.3.cloned.1.call-done = f32[1,128,128]{2,1,0:T(8,128)} async-done(((f32[16,128,128]{2,1,0:T(8,128)}), f32[1,128,128]{2,1,0:T(8,128)}) %reduce-scatter.3.cloned.1.call-update) | async-done | bytes 65552 | tf_op jit(solution)/shard_map/reduce_scatter | solution.py:81
  232.5 98.8 %all-gather.7.cloned.1.call-done = bf16[4096,172]{0,1:T(8,128)(2,1)} async-done(((bf16[128,172]{0,1:T(8,128)(2,1)}), bf16[4096,172]{0,1:T(8,128)(2,1)}) %all-gather.7.cloned.1.call-update) | async-done | bytes 1409040 | tf_op jit(solution)/shard_map/all_gather | solution.py:89
  331.3 3.8 copy.33
  335.8 26.3 %while.23 = (s32[]{:T(128)}, f32[16,128,172]{1,0,2:T(8,128)S(1)}, s32[]{:T(128)}, s32[128,2]{0,1:T(2,128)S(1)}, s32[]{:T(128)}, /*index=5*/bf16[128,128,128]{2,1...) while((s32[]{:T(128)}, f32[16,128,172]{1,0,2:T(8,128)S(1)}, ...), condition=%wide.region_4.5_spmd.clone, body=%wide.region_3.4_spmd.clone.sunk | while | flops 158516928 | bytes 8279115 | solution.py:56
  335.9 2.2 gather_fusion.1
  340.4 2.0 convolution_add_fusion.6
  342.4 2.2 gather_fusion.1
  346.9 2.0 convolution_add_fusion.6
  349.0 2.2 gather_fusion.1
  353.5 2.0 convolution_add_fusion.6
  355.6 2.2 gather_fusion.1
  360.1 2.0 convolution_add_fusion.6
  364.6 182.8 %all-reduce.3.cloned.1.call-done = f32[16,128,172]{1,0,2:T(8,128)} async-done(((f32[16,128,172]{1,0,2:T(8,128)}), f32[16,128,172]{1,0,2:T(8,128)}) %all-reduce.3.cloned.1.call-update) | async-done | bytes 1409040
  547.3 1.8 constant_dynamic-slice_fusion.2
  (86 shorter events, 28.9 us)
Async XLA Ops:
  7.2 224.5 %copy-start = (bf16[256,172]{0,1:T(8,128)(2,1)S(1)}, bf16[256,172]{0,1:T(8,128)(2,1)}, u32[]{:S(2)}) copy-start(bf16[256,172]{0,1:T(8,128)(2,1)} %param.22) | copy-start | bytes 264196
  7.2 98.7 %all-gather.5.cloned.1.call-start = ((), (), s32[]{:S(2)}) async-start(), calls=%async_computation.2 | async-start | bytes 1081344 | tf_op jit(solution)/shard_map/all_gather | solution.py:77
  7.9 222.7 %reduce-scatter.3.cloned.1.call-start = ((), (), s32[]{:S(2)}) async-start(), calls=%async_computation.1 | async-start | bytes 1114112 | tf_op jit(solution)/shard_map/reduce_scatter | solution.py:81
  132.2 1.5 copy-start.9
  132.2 98.4 %copy-start.3 = (bf16[1,1,128,128]{3,2,1,0:T(8,128)(2,1)S(1)}, bf16[1,1,128,128]{3,2,1,0:T(8,128)(2,1)}, u32[]{:S(2)}) copy-start(bf16[1,1,128,128]{3,2,1,0:T(8,128)(2,1)} %param.14) | copy-start | bytes 98308
  132.2 98.4 %copy-start.5 = (bf16[128,256]{1,0:T(8,128)(2,1)S(1)}, bf16[128,256]{1,0:T(8,128)(2,1)}, u32[]{:S(2)}) copy-start(bf16[128,256]{1,0:T(8,128)(2,1)} %param.20) | copy-start | bytes 196612
  132.2 98.4 %copy-start.6 = (bf16[1,1,128,256]{3,2,1,0:T(8,128)(2,1)S(1)}, bf16[1,1,128,256]{3,2,1,0:T(8,128)(2,1)}, u32[]{:S(2)}) copy-start(bf16[1,1,128,256]{3,2,1,0:T(8,128)(2,1)} %param.19) | copy-start | bytes 196612
  132.3 98.4 %copy-start.7 = (f32[256]{0:T(256)S(1)}, f32[256]{0:T(256)}, u32[]{:S(2)}) copy-start(f32[256]{0:T(256)} %param.21) | copy-start | bytes 3076
  133.6 197.7 %all-gather.7.cloned.1.call-start = ((), (), s32[]{:S(2)}) async-start(), calls=%async_computation.3 | async-start | bytes 1486848 | tf_op jit(solution)/shard_map/all_gather | solution.py:89
  231.6 103.5 %copy-start.2 = (bf16[128,256]{1,0:T(8,128)(2,1)}, bf16[128,256]{1,0:T(8,128)(2,1)S(1)}, u32[]{:S(2)}) copy-start(bf16[128,256]{1,0:T(8,128)(2,1)S(1)} %fusion.36) | copy-start | bytes 196612
  232.5 314.9 %all-reduce.3.cloned.1.call-start = ((), (), s32[]{:S(2)}) async-start(), calls=%async_computation.4 | async-start | bytes 2818048
  335.1 0.7 copy-start.4
  363.2 185.9 %copy-start.1 = (bf16[128,172]{0,1:T(8,128)(2,1)S(1)}, bf16[128,172]{0,1:T(8,128)(2,1)}, u32[]{:S(2)}) copy-start(bf16[128,172]{0,1:T(8,128)(2,1)} %convolution_convert_fusion) | copy-start | bytes 132100
  363.2 185.9 %copy-start.8 = (f32[172]{0:T(256)S(1)}, f32[172]{0:T(256)}, u32[]{:S(2)}) copy-start(f32[172]{0:T(256)} %param.23) | copy-start | bytes 2068
Sparse Core Ops, SparseCore 0:
  11.4 94.5 all-gather.4
  133.7 96.8 reduce-scatter.2
  234.8 96.4 all-gather.6
  363.4 183.8 all-reduce.2

commit v2 on v0

--- a/solution.py
+++ b/solution.py
@@ -1,7 +1,83 @@
+import functools
+
 import jax
 import jax.numpy as jnp
 from jax import lax
+from jax.experimental import pallas as pl
+from jax.experimental.pallas import tpu as pltpu
 from jax.sharding import PartitionSpec as P
+
+MESH_ID = pl.DeviceIdType.MESH
+
+
+def exchange_kernel(axis, other_axis, n, spread, src_ref, out_ref, send_sem, recv_sem):
+    me = lax.axis_index(axis)
+    other = lax.axis_index(other_axis)
+
+    def device(k):
+        return (k, other) if axis == "row" else (other, k)
+
+    def outgoing(k):
+        source = src_ref.at[k] if spread else src_ref
+        return pltpu.make_async_remote_copy(
+            src_ref=source,
+            dst_ref=out_ref.at[me],
+            send_sem=send_sem.at[k],
+            recv_sem=recv_sem.at[me],
+            device_id=device(k),
+            device_id_type=MESH_ID,
+        )
+
+    def incoming(k):
+        source = src_ref.at[k] if spread else src_ref
+        return pltpu.make_async_remote_copy(
+            src_ref=source,
+            dst_ref=out_ref.at[k],
+            send_sem=send_sem.at[k],
+            recv_sem=recv_sem.at[k],
+            device_id=device(k),
+            device_id_type=MESH_ID,
+        )
+
+    barrier = pltpu.get_barrier_semaphore()
+
+    def greet(step, carry):
+        k = lax.rem(me + step, n)
+        pl.semaphore_signal(barrier, 1, device_id=device(k), device_id_type=MESH_ID)
+        return carry
+
+    lax.fori_loop(1, n, greet, 0)
+    pl.semaphore_wait(barrier, n - 1)
+
+    def send(step, carry):
+        outgoing(lax.rem(me + step, n)).start()
+        return carry
+
+    lax.fori_loop(1, n, send, 0)
+    out_ref[me] = src_ref[me] if spread else src_ref[...]
+
+    def finish(step, carry):
+        k = lax.rem(me + step, n)
+        outgoing(k).wait_send()
+        incoming(lax.rem(me + n - step, n)).wait_recv()
+        return carry
+
+    lax.fori_loop(1, n, finish, 0)
+
+
+def exchange(block, axis, spread, tag):
+    other_axis = "col" if axis == "row" else "row"
+    n = lax.axis_size(axis)
+    shape = block.shape[1:] if spread else block.shape
+    vmem = pl.BlockSpec(memory_space=pltpu.VMEM)
+    return pl.pallas_call(
+        functools.partial(exchange_kernel, axis, other_axis, n, spread),
+        out_shape=jax.ShapeDtypeStruct((n, *shape), block.dtype),
+        in_specs=[vmem],
+        out_specs=vmem,
+        scratch_shapes=[pltpu.SemaphoreType.DMA((n,)), pltpu.SemaphoreType.DMA((n,))],
+        compiler_params=pltpu.CompilerParams(collective_id=tag, has_side_effects=True),
+    )(block)
 
 
 def joined_along(tiles, dim):
@@ -74,21 +150,23 @@
     slots = tile_set.shape[0]
     group_size = 16
     group_count = (live_total + group_size - 1) // group_size
-    gathered_input = collect(features[0], "row", 0)
+    gathered_input = exchange(features[0, 0], "row", False, 0)
     summed_one = tile_products(
         gathered_input, tile_set, coord_set, live_total, group_size, group_count
     )
-    owned_one = sent_and_summed(summed_one.astype(jnp.bfloat16), "col", 0)[0]
+    owned_one = exchange(summed_one.astype(jnp.bfloat16), "col", True, 1)
+    owned_one = owned_one.astype(jnp.float32).sum(axis=0)
     agg_one = (features[0, 0].astype(jnp.float32) + owned_one).astype(jnp.bfloat16)
     pre_one = jnp.dot(agg_one, weight_one, preferred_element_type=jnp.float32) + bias_one
     hidden = jax.nn.relu(pre_one).astype(jnp.bfloat16)
     pushed = jnp.where(batch_mask[0, 0][:, None] == 1, hidden, history[0, 0])
     projected = jnp.dot(pushed, weight_two, preferred_element_type=jnp.float32).astype(jnp.bfloat16)
-    gathered_proj = collect(projected[None], "row", 0)
+    gathered_proj = exchange(projected, "row", False, 2)
     summed_two = tile_products(
         gathered_proj, tile_set, coord_set, live_total, group_size, group_count
     )
-    owned_two = sent_and_summed(summed_two.astype(jnp.bfloat16), "col", 0)[0]
+    owned_two = exchange(summed_two.astype(jnp.bfloat16), "col", True, 3)
+    owned_two = owned_two.astype(jnp.float32).sum(axis=0)
     scores = projected.astype(jnp.float32) + owned_two + bias_two
     return (pushed[None, None], scores[None, None])
 

time: 236 us -> 263 us (1.11)
  the two profiles are of different devices: /device:TPU:8 before, /device:TPU:48 now
where the time goes in v2:
time: 263 us; the launch traced here: 262 us
  Pallas kernels  230 us (87%)
  matrix products  14.5 us (6%)
  local copies, waits for them, and re-layouts  9.56 us (4%)
  other arithmetic  6.01 us (2%)
    pallas_call x4, Pallas kernels, exchange(): pl.pallas_call(functools.partial(exchange_kernel, axis, other_axis, n, sp...  230 us
    dot_general x4, matrix products, one_group(): jnp.einsum('rg,gif->rif', placing, products, precision=lax.Precision.HIGH...  7.48 us
    dot_general x4, matrix products, one_group(): jnp.einsum('gij,gjf->gif', tile_group, sources, preferred_element_type=jn...  6.04 us
    gather x4, local copies, waits for them, and re-layouts, one_group(): sources = jnp.take(gathered, coord_group[:, 1], axis=0)  5.71 us

profile of v2, /device:TPU:48, one launch (start us, length us, event | category | flops | bytes accessed | tf_op | source)
XLA Modules:
  0.0 261.7 jit_solution(17637893558415383958)
XLA Ops:
  1.4 0.7 compare_bitcast_fusion
  2.0 39.1 %shard_map.113 = bf16[32,128,128]{2,1,0:T(8,128)(2,1)S(1)} custom-call(bf16[128,128]{1,0:T(8,128)(2,1)} %bitcast.51), custom_call_target="tpu_custom_call" | custom-call | tf_op jit(solution)/shard_map/pallas_call | solution.py:73
  41.2 9.3 %while.22 = (s32[]{:T(128)}, f32[16,128,128]{2,0,1:T(8,128)S(1)}, s32[]{:T(128)}, s32[128,2]{0,1:T(2,128)S(1)}, s32[]{:T(128)}, /*index=5*/bf16[128,128,128]{2,1...) while((s32[]{:T(128)}, f32[16,128,128]{2,0,1:T(8,128)S(1)}, ...), condition=%wide.region_1.2_spmd.clone, body=%wide.region_0.1_spmd.clone.sunk | while | flops 117966536 | bytes 6296651 | solution.py:132
  42.7 1.4 fusion.55
  44.1 1.8 convolution_add_fusion.5
  45.9 0.7 compare_convert_fusion.4
  47.3 1.4 fusion.55
  48.7 1.8 convolution_add_fusion.5
  50.6 1.1 copy.28.src_ref
  51.7 42.2 %shard_map.114 = bf16[16,128,128]{2,1,0:T(8,128)(2,1)} custom-call(bf16[16,128,128]{2,1,0:T(8,128)(2,1)} %copy.28.src_ref), custom_call_target="tpu_custom_call" | custom-call | tf_op jit(solution)/shard_map/pallas_call | solution.py:73
  93.9 1.1 convert_reduce_fusion.1
  95.2 0.8 convolution_convert_fusion.src_ref
  96.0 85.4 %shard_map.115 = bf16[32,128,172]{2,1,0:T(8,128)(2,1)} custom-call(bf16[128,172]{1,0:T(8,128)(2,1)} %convolution_convert_fusion.src_ref), custom_call_target="tpu_custom_call" | custom-call | tf_op jit(solution)/shard_map/pallas_call | solution.py:73
  181.5 13.2 %while.23 = (s32[]{:T(128)}, f32[16,128,172]{1,0,2:T(8,128)S(1)}, s32[]{:T(128)}, s32[128,2]{0,1:T(2,128)S(1)}, s32[]{:T(128)}, /*index=5*/bf16[128,128,128]{2,1...) while((s32[]{:T(128)}, f32[16,128,172]{1,0,2:T(8,128)S(1)}, ...), condition=%wide.region_4.5_spmd.clone, body=%wide.region_3.4_spmd.clone.sunk | while | flops 158516928 | bytes 8279115 | solution.py:132
  182.3 2.2 gather_fusion.1
  184.5 1.6 fusion.60
  186.1 2.0 convolution_add_fusion.6
  188.9 2.2 gather_fusion.1
  191.1 1.6 fusion.60
  192.7 2.0 convolution_add_fusion.6
  194.8 1.5 copy.18.src_ref
  196.2 63.2 %shard_map.116 = bf16[16,128,172]{2,1,0:T(8,128)(2,1)} custom-call(bf16[16,128,172]{2,1,0:T(8,128)(2,1)} %copy.18.src_ref), custom_call_target="tpu_custom_call" | custom-call | tf_op jit(solution)/shard_map/pallas_call | solution.py:73
  259.5 1.4 convert_reduce_fusion
  261.0 0.7 copy.19
  (44 shorter events, 4.1 us)
Async XLA Ops:
  0.6 94.6 %copy-start = (bf16[256,172]{0,1:T(8,128)(2,1)S(1)}, bf16[256,172]{0,1:T(8,128)(2,1)}, u32[]{:S(2)}) copy-start(bf16[256,172]{0,1:T(8,128)(2,1)} %param.22) | copy-start | bytes 264196
  0.6 40.6 %copy-start.4 = (s32[1,1,128,2]{2,3,1,0:T(2,128)S(1)}, s32[1,1,128,2]{2,3,1,0:T(2,128)}, u32[]{:S(2)}) copy-start(s32[1,1,128,2]{2,3,1,0:T(2,128)} %param.16) | copy-start | bytes 3076
  50.5 44.5 %copy-start.3 = (bf16[1,1,128,128]{3,2,1,0:T(8,128)(2,1)S(1)}, bf16[1,1,128,128]{3,2,1,0:T(8,128)(2,1)}, u32[]{:S(2)}) copy-start(bf16[1,1,128,128]{3,2,1,0:T(8,128)(2,1)} %param.14) | copy-start | bytes 98308
  50.5 44.5 %copy-start.5 = (bf16[128,256]{1,0:T(8,128)(2,1)S(1)}, bf16[128,256]{1,0:T(8,128)(2,1)}, u32[]{:S(2)}) copy-start(bf16[128,256]{1,0:T(8,128)(2,1)} %param.20) | copy-start | bytes 196612
  50.5 44.5 %copy-start.6 = (bf16[1,1,128,256]{3,2,1,0:T(8,128)(2,1)S(1)}, bf16[1,1,128,256]{3,2,1,0:T(8,128)(2,1)}, u32[]{:S(2)}) copy-start(bf16[1,1,128,256]{3,2,1,0:T(8,128)(2,1)} %param.19) | copy-start | bytes 196612
  50.6 44.5 %copy-start.7 = (f32[256]{0:T(256)S(1)}, f32[256]{0:T(256)}, u32[]{:S(2)}) copy-start(f32[256]{0:T(256)} %param.21) | copy-start | bytes 3076
  95.2 86.3 %copy-start.2 = (bf16[128,256]{1,0:T(8,128)(2,1)}, bf16[128,256]{1,0:T(8,128)(2,1)S(1)}, u32[]{:S(2)}) copy-start(bf16[128,256]{1,0:T(8,128)(2,1)S(1)} %fusion.36) | copy-start | bytes 196612
  196.2 64.7 %copy-start.1 = (bf16[128,172]{1,0:T(8,128)(2,1)S(1)}, bf16[128,172]{1,0:T(8,128)(2,1)}, u32[]{:S(2)}) copy-start(bf16[128,172]{1,0:T(8,128)(2,1)} %convolution_convert_fusion.src_ref) | copy-start | bytes 132100
  196.2 64.7 %copy-start.8 = (f32[172]{0:T(256)S(1)}, f32[172]{0:T(256)}, u32[]{:S(2)}) copy-start(f32[172]{0:T(256)} %param.23) | copy-start | bytes 2068

commit v3 on v2

--- a/solution.py
+++ b/solution.py
@@ -107,29 +107,64 @@
     return arrived.astype(jnp.float32).sum(axis=0)
 
 
-def tile_products(gathered, tiles, coords, live_total, group_size, group_count):
+def products_kernel(group, coords_ref, count_ref, tiles_ref, gathered_ref, out_ref, total_ref):
+    step = pl.program_id(0)
+
+    @pl.when(step == 0)
+    def _():
+        total_ref[...] = jnp.zeros_like(total_ref)
+
+    live = count_ref[0]
+
+    def one_tile(j, carry):
+        slot = step * group + j
+
+        @pl.when(slot < live)
+        def _():
+            target = coords_ref[2 * slot]
+            source = coords_ref[2 * slot + 1]
+            total_ref[target] += jnp.dot(
+                tiles_ref[j], gathered_ref[source], preferred_element_type=jnp.float32
+            )
+
+        return carry
+
+    @pl.when(step * group < live)
+    def _():
+        lax.fori_loop(0, group, one_tile, 0, unroll=True)
+
+    @pl.when(step == pl.num_programs(0) - 1)
+    def _():
+        out_ref[...] = total_ref[...].astype(out_ref.dtype)
+
+
+def tile_products(gathered, tiles, coords, live_total, group=16):
     row_blocks = lax.axis_size("col")
-    block_ids = jnp.arange(row_blocks, dtype=jnp.int32)
-
-    def one_group(step, running):
-        first = step * group_size
-        tile_group = lax.dynamic_slice_in_dim(tiles, first, group_size, 0)
-        coord_group = lax.dynamic_slice_in_dim(coords, first, group_size, 0)
-        sources = jnp.take(gathered, coord_group[:, 1], axis=0)
-        products = jnp.einsum(
-            "gij,gjf->gif", tile_group, sources, preferred_element_type=jnp.float32
-        )
-        slot_ids = first + jnp.arange(group_size, dtype=jnp.int32)
-        alive = (slot_ids < live_total).astype(jnp.float32)
-        placing = (coord_group[:, 0][None, :] == block_ids[:, None]).astype(jnp.float32) * alive[
-            None, :
-        ]
-        return running + jnp.einsum(
-            "rg,gif->rif", placing, products, precision=lax.Precision.HIGHEST
-        )
-
-    start_total = jnp.zeros((row_blocks, gathered.shape[1], gathered.shape[2]), jnp.float32)
-    return lax.fori_loop(0, group_count, one_group, start_total)
+    slots, size, _ = tiles.shape
+    width = gathered.shape[-1]
+    steps = slots // group
+
+    def tile_map(step, coords_ref, count_ref):
+        return (jnp.minimum(step, (count_ref[0] - 1) // group), 0, 0)
+
+    def whole(step, coords_ref, count_ref):
+        return (0, 0, 0)
+
+    grid_spec = pltpu.PrefetchScalarGridSpec(
+        num_scalar_prefetch=2,
+        grid=(steps,),
+        in_specs=[
+            pl.BlockSpec((group, size, size), tile_map),
+            pl.BlockSpec(gathered.shape, whole),
+        ],
+        out_specs=pl.BlockSpec((row_blocks, size, width), whole),
+        scratch_shapes=[pltpu.VMEM((row_blocks, size, width), jnp.float32)],
+    )
+    return pl.pallas_call(
+        functools.partial(products_kernel, group),
+        grid_spec=grid_spec,
+        out_shape=jax.ShapeDtypeStruct((row_blocks, size, width), jnp.bfloat16),
+    )(coords.reshape(-1), live_total.reshape(1), tiles, gathered)
 
 
 def on_device(
@@ -147,14 +182,9 @@
     tile_set = tiles[0, 0]
     coord_set = tile_coords[0, 0]
     live_total = tile_count[0, 0]
-    slots = tile_set.shape[0]
-    group_size = 16
-    group_count = (live_total + group_size - 1) // group_size
     gathered_input = exchange(features[0, 0], "row", False, 0)
-    summed_one = tile_products(
-        gathered_input, tile_set, coord_set, live_total, group_size, group_count
-    )
-    owned_one = exchange(summed_one.astype(jnp.bfloat16), "col", True, 1)
+    summed_one = tile_products(gathered_input, tile_set, coord_set, live_total)
+    owned_one = exchange(summed_one, "col", True, 1)
     owned_one = owned_one.astype(jnp.float32).sum(axis=0)
     agg_one = (features[0, 0].astype(jnp.float32) + owned_one).astype(jnp.bfloat16)
     pre_one = jnp.dot(agg_one, weight_one, preferred_element_type=jnp.float32) + bias_one
@@ -162,10 +192,8 @@
     pushed = jnp.where(batch_mask[0, 0][:, None] == 1, hidden, history[0, 0])
     projected = jnp.dot(pushed, weight_two, preferred_element_type=jnp.float32).astype(jnp.bfloat16)
     gathered_proj = exchange(projected, "row", False, 2)
-    summed_two = tile_products(
-        gathered_proj, tile_set, coord_set, live_total, group_size, group_count
-    )
-    owned_two = exchange(summed_two.astype(jnp.bfloat16), "col", True, 3)
+    summed_two = tile_products(gathered_proj, tile_set, coord_set, live_total)
+    owned_two = exchange(summed_two, "col", True, 3)
     owned_two = owned_two.astype(jnp.float32).sum(axis=0)
     scores = projected.astype(jnp.float32) + owned_two + bias_two
     return (pushed[None, None], scores[None, None])

time: 263 us -> 220 us (0.84)
  the two profiles are of different devices: /device:TPU:48 before, /device:TPU:49 now
where the time goes in v3:
time: 220 us; the launch traced here: 219 us
  Pallas kernels  211 us (96%)
  other arithmetic  3.21 us (1%)
  local copies, waits for them, and re-layouts  2.23 us (1%)
    pallas_call x4, Pallas kernels, exchange(): pl.pallas_call(functools.partial(exchange_kernel, axis, other_axis, n, sp...  188 us
    pallas_call x2, Pallas kernels, tile_products(): pl.pallas_call(functools.partial(products_kernel, group), grid_spec=grid_...  23.5 us

profile of v3, /device:TPU:49, one launch (start us, length us, event | category | flops | bytes accessed | tf_op | source)
XLA Modules:
  0.0 218.9 jit_solution(17924093903672975116)
XLA Ops:
  0.6 0.0 copy-start
  1.3 0.7 compare_bitcast_fusion
  2.0 0.8 copy.14
  2.8 0.7 reshape_squeeze.8.coords_ref
  3.4 40.5 %shard_map.113.gathered_ref = bf16[32,128,128]{2,1,0:T(8,128)(2,1)} custom-call(bf16[128,128]{1,0:T(8,128)(2,1)} %bitcast.24), custom_call_target="tpu_custom_call" | custom-call | tf_op jit(solution)/shard_map/pallas_call | solution.py:73
  43.9 0.0 copy-start.3
  43.9 0.0 copy-start.4
  43.9 0.0 copy-start.5
  43.9 0.0 copy-start.6
  43.9 11.0 %shard_map.114.src_ref = bf16[16,128,128]{2,1,0:T(8,128)(2,1)} custom-call(s32[256]{0:T(256)} %reshape_squeeze.8.coords_ref, s32[1]{0:T(128)} %bitcast.19.count_ref, bf16[128,128,128]{2,1,0:T(8,128)(2,1)} %bitcast.21, bf16[32,128,128]{2,1,0:T(8,128)(2,1)} %shard_map.113.gathered_ref), custom_call_target="tpu_custom_call" | custom-call | tf_op jit(solution)/shard_map/pallas_call | solution.py:163
  54.9 24.4 %shard_map.115 = bf16[16,128,128]{2,1,0:T(8,128)(2,1)} custom-call(bf16[16,128,128]{2,1,0:T(8,128)(2,1)} %shard_map.114.src_ref), custom_call_target="tpu_custom_call" | custom-call | tf_op jit(solution)/shard_map/pallas_call | solution.py:73
  79.4 1.1 convert_reduce_fusion.1
  80.5 0.0 copy-done.3
  80.5 0.0 copy-done.4
  80.5 0.0 copy-done.5
  80.5 0.0 copy-done.6
  80.5 0.2 fusion.2
  80.7 0.0 copy-start.2
  80.7 0.8 convolution_convert_fusion.src_ref
  81.5 76.6 %shard_map.116.gathered_ref = bf16[32,128,172]{2,1,0:T(8,128)(2,1)} custom-call(bf16[128,172]{1,0:T(8,128)(2,1)} %convolution_convert_fusion.src_ref), custom_call_target="tpu_custom_call" | custom-call | tf_op jit(solution)/shard_map/pallas_call | solution.py:73
  158.2 12.5 %shard_map.117.src_ref = bf16[16,128,172]{2,1,0:T(8,128)(2,1)} custom-call(s32[256]{0:T(256)} %reshape_squeeze.8.coords_ref, s32[1]{0:T(128)} %bitcast.20.count_ref, bf16[128,128,128]{2,1,0:T(8,128)(2,1)} %bitcast.22, bf16[32,128,172]{2,1,0:T(8,128)(2,1)} %shard_map.116.gathered_ref), custom_call_target="tpu_custom_call" | custom-call | tf_op jit(solution)/shard_map/pallas_call | solution.py:163
  170.7 46.1 %shard_map.118 = bf16[16,128,172]{2,1,0:T(8,128)(2,1)} custom-call(bf16[16,128,172]{2,1,0:T(8,128)(2,1)} %shard_map.117.src_ref), custom_call_target="tpu_custom_call" | custom-call | tf_op jit(solution)/shard_map/pallas_call | solution.py:73
  216.7 1.4 convert_reduce_fusion
  218.2 0.7 copy.16
  (7 shorter events, 0.0 us)
Async XLA Ops:
  0.6 80.1 %copy-start = (bf16[256,172]{0,1:T(8,128)(2,1)S(1)}, bf16[256,172]{0,1:T(8,128)(2,1)}, u32[]{:S(2)}) copy-start(bf16[256,172]{0,1:T(8,128)(2,1)} %param.18) | copy-start | bytes 264196
  43.9 36.6 %copy-start.3 = (bf16[1,1,128,128]{3,2,1,0:T(8,128)(2,1)S(1)}, bf16[1,1,128,128]{3,2,1,0:T(8,128)(2,1)}, u32[]{:S(2)}) copy-start(bf16[1,1,128,128]{3,2,1,0:T(8,128)(2,1)} %param.10) | copy-start | bytes 98308
  43.9 36.6 %copy-start.4 = (bf16[128,256]{1,0:T(8,128)(2,1)S(1)}, bf16[128,256]{1,0:T(8,128)(2,1)}, u32[]{:S(2)}) copy-start(bf16[128,256]{1,0:T(8,128)(2,1)} %param.16) | copy-start | bytes 196612
  43.9 36.6 %copy-start.5 = (bf16[1,1,128,256]{3,2,1,0:T(8,128)(2,1)S(1)}, bf16[1,1,128,256]{3,2,1,0:T(8,128)(2,1)}, u32[]{:S(2)}) copy-start(bf16[1,1,128,256]{3,2,1,0:T(8,128)(2,1)} %param.15) | copy-start | bytes 196612
  43.9 36.6 %copy-start.6 = (f32[256]{0:T(256)S(1)}, f32[256]{0:T(256)}, u32[]{:S(2)}) copy-start(f32[256]{0:T(256)} %param.17) | copy-start | bytes 3076
  80.7 90.0 %copy-start.2 = (bf16[128,256]{1,0:T(8,128)(2,1)}, bf16[128,256]{1,0:T(8,128)(2,1)S(1)}, u32[]{:S(2)}) copy-start(bf16[128,256]{1,0:T(8,128)(2,1)S(1)} %fusion.2) | copy-start | bytes 196612
  170.7 47.5 %copy-start.1 = (bf16[128,172]{1,0:T(8,128)(2,1)S(1)}, bf16[128,172]{1,0:T(8,128)(2,1)}, u32[]{:S(2)}) copy-start(bf16[128,172]{1,0:T(8,128)(2,1)} %convolution_convert_fusion.src_ref) | copy-start | bytes 132100
  170.7 47.5 %copy-start.7 = (f32[172]{0:T(256)S(1)}, f32[172]{0:T(256)}, u32[]{:S(2)}) copy-start(f32[172]{0:T(256)} %param.19) | copy-start | bytes 2068

commit v4 on v3

--- a/solution.py
+++ b/solution.py
@@ -191,10 +191,13 @@
     hidden = jax.nn.relu(pre_one).astype(jnp.bfloat16)
     pushed = jnp.where(batch_mask[0, 0][:, None] == 1, hidden, history[0, 0])
     projected = jnp.dot(pushed, weight_two, preferred_element_type=jnp.float32).astype(jnp.bfloat16)
-    gathered_proj = exchange(projected, "row", False, 2)
+    nodes, classes = projected.shape
+    dense = projected.reshape(classes, nodes)
+    gathered_proj = exchange(dense, "row", False, 2).reshape(-1, nodes, classes)
     summed_two = tile_products(gathered_proj, tile_set, coord_set, live_total)
-    owned_two = exchange(summed_two, "col", True, 3)
-    owned_two = owned_two.astype(jnp.float32).sum(axis=0)
+    dense_two = summed_two.reshape(summed_two.shape[0], classes, nodes)
+    owned_two = exchange(dense_two, "col", True, 3).astype(jnp.float32).sum(axis=0)
+    owned_two = owned_two.reshape(nodes, classes)
     scores = projected.astype(jnp.float32) + owned_two + bias_two
     return (pushed[None, None], scores[None, None])
 

time: 220 us -> 199 us (0.905)
  the two profiles are of different devices: /device:TPU:49 before, /device:TPU:48 now
where the time goes in v4:
time: 199 us; the launch traced here: 198 us
  Pallas kernels  178 us (89%)
  local copies, waits for them, and re-layouts  15.4 us (8%)
  other arithmetic  3.09 us (2%)
    pallas_call x4, Pallas kernels, exchange(): pl.pallas_call(functools.partial(exchange_kernel, axis, other_axis, n, sp...  135 us
    pallas_call x2, Pallas kernels, tile_products(): pl.pallas_call(functools.partial(products_kernel, group), grid_spec=grid_...  43.3 us
    reshape x1, local copies, waits for them, and re-layouts, on_device(): gathered_proj = exchange(dense, 'row', False, 2).reshape(-1, nodes, classes)  7.84 us
    reshape x1, local copies, waits for them, and re-layouts, on_device(): dense_two = summed_two.reshape(summed_two.shape[0], classes, nodes)  4.22 us

profile of v4, /device:TPU:48, one launch (start us, length us, event | category | flops | bytes accessed | tf_op | source)
XLA Modules:
  0.0 198.3 jit_solution(12820877473518312326)
XLA Ops:
  0.6 0.0 copy-start
  1.3 0.7 compare_bitcast_fusion
  2.0 0.8 copy.14
  2.8 0.7 reshape_squeeze.8.coords_ref
  3.4 40.1 %shard_map.113.gathered_ref = bf16[32,128,128]{2,1,0:T(8,128)(2,1)} custom-call(bf16[128,128]{1,0:T(8,128)(2,1)} %bitcast.24), custom_call_target="tpu_custom_call" | custom-call | tf_op jit(solution)/shard_map/pallas_call | solution.py:73
  43.5 0.0 copy-start.2
  43.6 20.5 %shard_map.114.src_ref = bf16[16,128,128]{2,1,0:T(8,128)(2,1)} custom-call(s32[256]{0:T(256)} %reshape_squeeze.8.coords_ref, s32[1]{0:T(128)} %bitcast.19.count_ref, bf16[128,128,128]{2,1,0:T(8,128)(2,1)} %bitcast.21, bf16[32,128,128]{2,1,0:T(8,128)(2,1)} %shard_map.113.gathered_ref), custom_call_target="tpu_custom_call" | custom-call | tf_op jit(solution)/shard_map/pallas_call | solution.py:163
  64.0 19.3 %shard_map.115 = bf16[16,128,128]{2,1,0:T(8,128)(2,1)} custom-call(bf16[16,128,128]{2,1,0:T(8,128)(2,1)} %shard_map.114.src_ref), custom_call_target="tpu_custom_call" | custom-call | tf_op jit(solution)/shard_map/pallas_call | solution.py:73
  83.3 1.1 convert_reduce_fusion.1
  84.5 0.2 fusion.2
  84.6 0.0 copy-start.1
  84.6 0.2 convolution_convert_fusion
  84.8 0.1 copy.15
  84.9 0.8 reshape.27.src_ref
  85.7 54.1 %shard_map.116 = bf16[32,172,128]{2,1,0:T(8,128)(2,1)} custom-call(bf16[172,128]{1,0:T(8,128)(2,1)} %reshape.27.src_ref), custom_call_target="tpu_custom_call" | custom-call | tf_op jit(solution)/shard_map/pallas_call | solution.py:73
  139.8 7.8 %reshape.28.gathered_ref = bf16[32,128,172]{2,1,0:T(8,128)(2,1)} reshape(bf16[32,172,128]{2,1,0:T(8,128)(2,1)} %shard_map.116) | data formatting | bytes 2818048 | tf_op jit(solution)/shard_map/reshape | solution.py:196
  147.6 22.8 %shard_map.117 = bf16[16,128,172]{2,1,0:T(8,128)(2,1)} custom-call(s32[256]{0:T(256)} %reshape_squeeze.8.coords_ref, s32[1]{0:T(128)} %bitcast.20.count_ref, bf16[128,128,128]{2,1,0:T(8,128)(2,1)} %bitcast.22, bf16[32,128,172]{2,1,0:T(8,128)(2,1)} %reshape.28.gathered_ref), custom_call_target="tpu_custom_call" | custom-call | tf_op jit(solution)/shard_map/pallas_call | solution.py:163
  170.5 4.2 %reshape.29.src_ref = bf16[16,172,128]{2,1,0:T(8,128)(2,1)} reshape(bf16[16,128,172]{2,1,0:T(8,128)(2,1)} %shard_map.117) | data formatting | bytes 1409024 | tf_op jit(solution)/shard_map/reshape | solution.py:198
  174.7 21.3 %shard_map.118 = bf16[16,172,128]{2,1,0:T(8,128)(2,1)} custom-call(bf16[16,172,128]{2,1,0:T(8,128)(2,1)} %reshape.29.src_ref), custom_call_target="tpu_custom_call" | custom-call | tf_op jit(solution)/shard_map/pallas_call | solution.py:73
  196.0 1.2 convert_reduce_fusion
  197.2 0.2 reshape.30
  197.4 0.1 copy.16
  197.5 0.1 add_bitcast_fusion
  197.6 0.7 copy.17
  (11 shorter events, 0.0 us)
Async XLA Ops:
  0.6 84.0 %copy-start = (bf16[256,172]{0,1:T(8,128)(2,1)S(1)}, bf16[256,172]{0,1:T(8,128)(2,1)}, u32[]{:S(2)}) copy-start(bf16[256,172]{0,1:T(8,128)(2,1)} %param.18) | copy-start | bytes 264196
  43.5 40.9 %copy-start.2 = (bf16[1,1,128,128]{3,2,1,0:T(8,128)(2,1)S(1)}, bf16[1,1,128,128]{3,2,1,0:T(8,128)(2,1)}, u32[]{:S(2)}) copy-start(bf16[1,1,128,128]{3,2,1,0:T(8,128)(2,1)} %param.10) | copy-start | bytes 98308
  43.5 40.9 %copy-start.3 = (bf16[128,256]{1,0:T(8,128)(2,1)S(1)}, bf16[128,256]{1,0:T(8,128)(2,1)}, u32[]{:S(2)}) copy-start(bf16[128,256]{1,0:T(8,128)(2,1)} %param.16) | copy-start | bytes 196612
  43.5 40.9 %copy-start.4 = (bf16[1,1,128,256]{3,2,1,0:T(8,128)(2,1)S(1)}, bf16[1,1,128,256]{3,2,1,0:T(8,128)(2,1)}, u32[]{:S(2)}) copy-start(bf16[1,1,128,256]{3,2,1,0:T(8,128)(2,1)} %param.15) | copy-start | bytes 196612
  43.5 40.9 %copy-start.5 = (f32[256]{0:T(256)S(1)}, f32[256]{0:T(256)}, u32[]{:S(2)}) copy-start(f32[256]{0:T(256)} %param.17) | copy-start | bytes 3076
  84.6 63.0 %copy-start.1 = (bf16[128,256]{1,0:T(8,128)(2,1)}, bf16[128,256]{1,0:T(8,128)(2,1)S(1)}, u32[]{:S(2)}) copy-start(bf16[128,256]{1,0:T(8,128)(2,1)S(1)} %fusion.2) | copy-start | bytes 196612
  170.5 27.0 %copy-start.6 = (f32[172]{0:T(256)S(1)}, f32[172]{0:T(256)}, u32[]{:S(2)}) copy-start(f32[172]{0:T(256)} %param.19) | copy-start | bytes 2068

commit v5 on v3

--- a/solution.py
+++ b/solution.py
@@ -107,7 +107,7 @@
     return arrived.astype(jnp.float32).sum(axis=0)
 
 
-def products_kernel(group, coords_ref, count_ref, tiles_ref, gathered_ref, out_ref, total_ref):
+def products_kernel(group, flipped, coords_ref, count_ref, tiles_ref, gathered_ref, out_ref, total_ref):
     step = pl.program_id(0)
 
     @pl.when(step == 0)
@@ -123,9 +123,18 @@
         def _():
             target = coords_ref[2 * slot]
             source = coords_ref[2 * slot + 1]
-            total_ref[target] += jnp.dot(
-                tiles_ref[j], gathered_ref[source], preferred_element_type=jnp.float32
-            )
+            if flipped:
+                product = lax.dot_general(
+                    gathered_ref[source],
+                    tiles_ref[j],
+                    (((1,), (1,)), ((), ())),
+                    preferred_element_type=jnp.float32,
+                )
+            else:
+                product = jnp.dot(
+                    tiles_ref[j], gathered_ref[source], preferred_element_type=jnp.float32
+                )
+            total_ref[target] += product
 
         return carry
 
@@ -138,10 +147,10 @@
         out_ref[...] = total_ref[...].astype(out_ref.dtype)
 
 
-def tile_products(gathered, tiles, coords, live_total, group=16):
+def tile_products(gathered, tiles, coords, live_total, flipped=False, group=16):
     row_blocks = lax.axis_size("col")
     slots, size, _ = tiles.shape
-    width = gathered.shape[-1]
+    block_shape = gathered.shape[1:]
     steps = slots // group
 
     def tile_map(step, coords_ref, count_ref):
@@ -157,13 +166,13 @@
             pl.BlockSpec((group, size, size), tile_map),
             pl.BlockSpec(gathered.shape, whole),
         ],
-        out_specs=pl.BlockSpec((row_blocks, size, width), whole),
-        scratch_shapes=[pltpu.VMEM((row_blocks, size, width), jnp.float32)],
+        out_specs=pl.BlockSpec((row_blocks, *block_shape), whole),
+        scratch_shapes=[pltpu.VMEM((row_blocks, *block_shape), jnp.float32)],
     )
     return pl.pallas_call(
-        functools.partial(products_kernel, group),
+        functools.partial(products_kernel, group, flipped),
         grid_spec=grid_spec,
-        out_shape=jax.ShapeDtypeStruct((row_blocks, size, width), jnp.bfloat16),
+        out_shape=jax.ShapeDtypeStruct((row_blocks, *block_shape), jnp.bfloat16),
     )(coords.reshape(-1), live_total.reshape(1), tiles, gathered)
 
 
@@ -191,10 +200,9 @@
     hidden = jax.nn.relu(pre_one).astype(jnp.bfloat16)
     pushed = jnp.where(batch_mask[0, 0][:, None] == 1, hidden, history[0, 0])
     projected = jnp.dot(pushed, weight_two, preferred_element_type=jnp.float32).astype(jnp.bfloat16)
-    gathered_proj = exchange(projected, "row", False, 2)
-    summed_two = tile_products(gathered_proj, tile_set, coord_set, live_total)
-    owned_two = exchange(summed_two, "col", True, 3)
-    owned_two = owned_two.astype(jnp.float32).sum(axis=0)
+    gathered_proj = exchange(projected.T, "row", False, 2)
+    summed_two = tile_products(gathered_proj, tile_set, coord_set, live_total, True)
+    owned_two = exchange(summed_two, "col", True, 3).astype(jnp.float32).sum(axis=0).T
     scores = projected.astype(jnp.float32) + owned_two + bias_two
     return (pushed[None, None], scores[None, None])
 

time: 220 us -> 177 us (0.80)
  the two profiles are of different devices: /device:TPU:49 before, /device:TPU:1 now
where the time goes in v5:
time: 177 us; the launch traced here: 175 us
  Pallas kernels  167 us (94%)
  other arithmetic  3.09 us (2%)
  local copies, waits for them, and re-layouts  2.27 us (1%)
    pallas_call x4, Pallas kernels, exchange(): pl.pallas_call(functools.partial(exchange_kernel, axis, other_axis, n, sp...  152 us
    pallas_call x2, Pallas kernels, tile_products(): pl.pallas_call(functools.partial(products_kernel, group, flipped), grid_s...  15.4 us

profile of v5, /device:TPU:1, one launch (start us, length us, event | category | flops | bytes accessed | tf_op | source)
XLA Modules:
  0.0 175.3 jit_solution(3687594680989911469)
XLA Ops:
  0.6 0.0 copy-start
  1.3 0.7 compare_bitcast_fusion
  2.0 0.8 copy.13
  2.8 0.7 reshape_squeeze.8.coords_ref
  3.5 43.0 %shard_map.113.gathered_ref = bf16[32,128,128]{2,1,0:T(8,128)(2,1)} custom-call(bf16[128,128]{1,0:T(8,128)(2,1)} %bitcast.32), custom_call_target="tpu_custom_call" | custom-call | tf_op jit(solution)/shard_map/pallas_call | solution.py:73
  46.5 6.9 %shard_map.114.src_ref = bf16[16,128,128]{2,1,0:T(8,128)(2,1)} custom-call(s32[256]{0:T(256)} %reshape_squeeze.8.coords_ref, s32[1]{0:T(128)} %bitcast.26.count_ref, bf16[128,128,128]{2,1,0:T(8,128)(2,1)} %bitcast.28, bf16[32,128,128]{2,1,0:T(8,128)(2,1)} %shard_map.113.gathered_ref), custom_call_target="tpu_custom_call" | custom-call | tf_op jit(solution)/shard_map/pallas_call | solution.py:172
  53.4 21.4 %shard_map.115 = bf16[16,128,128]{2,1,0:T(8,128)(2,1)} custom-call(bf16[16,128,128]{2,1,0:T(8,128)(2,1)} %shard_map.114.src_ref), custom_call_target="tpu_custom_call" | custom-call | tf_op jit(solution)/shard_map/pallas_call | solution.py:73
  74.8 1.1 convert_reduce_fusion.1
  75.9 0.0 copy-done.3
  75.9 0.0 copy-done.4
  75.9 0.0 copy-done.5
  75.9 0.0 copy-done.6
  75.9 0.2 fusion.2
  76.1 0.0 copy-start.2
  76.1 0.0 copy-done
  76.1 0.8 convolution_convert_fusion
  76.9 56.1 %shard_map.116.gathered_ref = bf16[32,172,128]{2,1,0:T(8,128)(2,1)} custom-call(bf16[172,128]{1,0:T(8,128)(2,1)} %bitcast.30), custom_call_target="tpu_custom_call" | custom-call | tf_op jit(solution)/shard_map/pallas_call | solution.py:73
  133.0 8.4 %shard_map.117.src_ref = bf16[16,172,128]{2,1,0:T(8,128)(2,1)} custom-call(s32[256]{0:T(256)} %reshape_squeeze.8.coords_ref, s32[1]{0:T(128)} %bitcast.27.count_ref, bf16[128,128,128]{2,1,0:T(8,128)(2,1)} %bitcast.29, bf16[32,172,128]{2,1,0:T(8,128)(2,1)} %shard_map.116.gathered_ref), custom_call_target="tpu_custom_call" | custom-call | tf_op jit(solution)/shard_map/pallas_call | solution.py:172
  141.5 0.0 copy-done.2
  141.5 31.7 %shard_map.118 = bf16[16,172,128]{2,1,0:T(8,128)(2,1)} custom-call(bf16[16,172,128]{2,1,0:T(8,128)(2,1)} %shard_map.117.src_ref), custom_call_target="tpu_custom_call" | custom-call | tf_op jit(solution)/shard_map/pallas_call | solution.py:73
  173.2 1.2 convert_reduce_fusion
  174.4 0.0 copy-done.1
  174.4 0.1 fusion.4
  174.5 0.7 copy.14
  (7 shorter events, 0.0 us)
Async XLA Ops:
  0.6 75.5 %copy-start = (bf16[256,172]{0,1:T(8,128)(2,1)S(1)}, bf16[256,172]{0,1:T(8,128)(2,1)}, u32[]{:S(2)}) copy-start(bf16[256,172]{0,1:T(8,128)(2,1)} %param.18) | copy-start | bytes 264196
  53.4 22.5 %copy-start.3 = (bf16[1,1,128,128]{3,2,1,0:T(8,128)(2,1)S(1)}, bf16[1,1,128,128]{3,2,1,0:T(8,128)(2,1)}, u32[]{:S(2)}) copy-start(bf16[1,1,128,128]{3,2,1,0:T(8,128)(2,1)} %param.10) | copy-start | bytes 98308
  53.4 22.5 %copy-start.4 = (bf16[128,256]{1,0:T(8,128)(2,1)S(1)}, bf16[128,256]{1,0:T(8,128)(2,1)}, u32[]{:S(2)}) copy-start(bf16[128,256]{1,0:T(8,128)(2,1)} %param.16) | copy-start | bytes 196612
  53.4 22.5 %copy-start.5 = (bf16[1,1,128,256]{3,2,1,0:T(8,128)(2,1)S(1)}, bf16[1,1,128,256]{3,2,1,0:T(8,128)(2,1)}, u32[]{:S(2)}) copy-start(bf16[1,1,128,256]{3,2,1,0:T(8,128)(2,1)} %param.15) | copy-start | bytes 196612
  53.4 22.5 %copy-start.6 = (f32[256]{0:T(256)S(1)}, f32[256]{0:T(256)}, u32[]{:S(2)}) copy-start(f32[256]{0:T(256)} %param.17) | copy-start | bytes 3076
  76.1 65.4 %copy-start.2 = (bf16[128,256]{1,0:T(8,128)(2,1)}, bf16[128,256]{1,0:T(8,128)(2,1)S(1)}, u32[]{:S(2)}) copy-start(bf16[128,256]{1,0:T(8,128)(2,1)S(1)} %fusion.2) | copy-start | bytes 196612
  141.5 32.9 %copy-start.1 = (bf16[128,172]{0,1:T(8,128)(2,1)S(1)}, bf16[128,172]{0,1:T(8,128)(2,1)}, u32[]{:S(2)}) copy-start(bf16[128,172]{0,1:T(8,128)(2,1)} %convolution_convert_fusion) | copy-start | bytes 132100
  141.5 32.9 %copy-start.7 = (f32[172]{0:T(256)S(1)}, f32[172]{0:T(256)}, u32[]{:S(2)}) copy-start(f32[172]{0:T(256)} %param.19) | copy-start | bytes 2068

commit v6 on v5

--- a/solution.py
+++ b/solution.py
@@ -63,6 +63,79 @@
         return carry
 
     lax.fori_loop(1, n, finish, 0)
+
+
+def gather_kernel(n, src_ref, out_ref, send_sem, pass_sem, recv_sem):
+    me = lax.axis_index("row")
+    other = lax.axis_index("col")
+    twin = me + 1 - 2 * lax.rem(me, 2)
+    half = n // 2
+
+    def copy(source, slot, sems, k):
+        return pltpu.make_async_remote_copy(
+            src_ref=source,
+            dst_ref=out_ref.at[slot],
+            send_sem=sems.at[k],
+            recv_sem=recv_sem.at[slot],
+            device_id=(k, other),
+            device_id_type=MESH_ID,
+        )
+
+    def peer(step):
+        return lax.rem(me + 2 * step, n)
+
+    def far(step):
+        return lax.rem(twin + 2 * step, n)
+
+    barrier = pltpu.get_barrier_semaphore()
+    pl.semaphore_signal(barrier, 1, device_id=(twin, other), device_id_type=MESH_ID)
+
+    def greet(step, carry):
+        pl.semaphore_signal(barrier, 1, device_id=(peer(step), other), device_id_type=MESH_ID)
+        return carry
+
+    lax.fori_loop(1, half, greet, 0)
+    pl.semaphore_wait(barrier, half)
+
+    def send(step, carry):
+        copy(src_ref, me, send_sem, peer(step)).start()
+        return carry
+
+    lax.fori_loop(1, half, send, 0)
+    copy(src_ref, me, send_sem, twin).start()
+    out_ref[me] = src_ref[...]
+
+    def relay(step, carry):
+        k = peer(step)
+        copy(src_ref, k, send_sem, k).wait_recv()
+        copy(out_ref.at[k], k, pass_sem, twin).start()
+        return carry
+
+    lax.fori_loop(1, half, relay, 0)
+
+    def finish(step, carry):
+        k = peer(step)
+        copy(src_ref, me, send_sem, k).wait_send()
+        copy(out_ref.at[k], k, pass_sem, twin).wait_send()
+        copy(src_ref, far(step), send_sem, twin).wait_recv()
+        return carry
+
+    lax.fori_loop(1, half, finish, 0)
+    copy(src_ref, me, send_sem, twin).wait_send()
+    copy(src_ref, twin, send_sem, twin).wait_recv()
+
+
+def gather(block, tag):
+    n = lax.axis_size("row")
+    vmem = pl.BlockSpec(memory_space=pltpu.VMEM)
+    return pl.pallas_call(
+        functools.partial(gather_kernel, n),
+        out_shape=jax.ShapeDtypeStruct((n, *block.shape), block.dtype),
+        in_specs=[vmem],
+        out_specs=vmem,
+        scratch_shapes=[pltpu.SemaphoreType.DMA((n,))] * 3,
+        compiler_params=pltpu.CompilerParams(collective_id=tag, has_side_effects=True),
+    )(block)
 
 
 def exchange(block, axis, spread, tag):
@@ -191,7 +264,7 @@
     tile_set = tiles[0, 0]
     coord_set = tile_coords[0, 0]
     live_total = tile_count[0, 0]
-    gathered_input = exchange(features[0, 0], "row", False, 0)
+    gathered_input = gather(features[0, 0], 0)
     summed_one = tile_products(gathered_input, tile_set, coord_set, live_total)
     owned_one = exchange(summed_one, "col", True, 1)
     owned_one = owned_one.astype(jnp.float32).sum(axis=0)
@@ -200,7 +273,7 @@
     hidden = jax.nn.relu(pre_one).astype(jnp.bfloat16)
     pushed = jnp.where(batch_mask[0, 0][:, None] == 1, hidden, history[0, 0])
     projected = jnp.dot(pushed, weight_two, preferred_element_type=jnp.float32).astype(jnp.bfloat16)
-    gathered_proj = exchange(projected.T, "row", False, 2)
+    gathered_proj = gather(projected.T, 2)
     summed_two = tile_products(gathered_proj, tile_set, coord_set, live_total, True)
     owned_two = exchange(summed_two, "col", True, 3).astype(jnp.float32).sum(axis=0).T
     scores = projected.astype(jnp.float32) + owned_two + bias_two

time: 177 us -> 152 us (0.86)
  Pallas kernels: 167 us -> 142 us
    pallas_call x4 -> x2, Pallas kernels: 152 us -> 64.1 us  [exchange(): pl.pallas_call(functools.partial(exchange_kernel, axis, other_axis, n, sp...]
    pallas_call x0 -> x2, Pallas kernels: none -> 68.7 us  [gather(): pl.pallas_call(functools.partial(gather_kernel, n), out_shape=jax.ShapeDt...]
    pallas_call x2, Pallas kernels: 15.4 us -> 8.8 us  [tile_products(): pl.pallas_call(functools.partial(products_kernel, group, flipped), grid_s...]
where the time goes in v6:
time: 152 us; the launch traced here: 149 us
  Pallas kernels  142 us (93%)
  other arithmetic  3.09 us (2%)
  local copies, waits for them, and re-layouts  2.27 us (1%)
    pallas_call x2, Pallas kernels, gather(): pl.pallas_call(functools.partial(gather_kernel, n), out_shape=jax.ShapeDt...  68.7 us
    pallas_call x2, Pallas kernels, exchange(): pl.pallas_call(functools.partial(exchange_kernel, axis, other_axis, n, sp...  64.1 us
    pallas_call x2, Pallas kernels, tile_products(): pl.pallas_call(functools.partial(products_kernel, group, flipped), grid_s...  8.8 us

profile of v6, /device:TPU:1, one launch (start us, length us, event | category | flops | bytes accessed | tf_op | source)
XLA Modules:
  0.0 149.3 jit_solution(5296219476188608587)
XLA Ops:
  0.6 0.0 copy-start
  1.3 0.7 compare_bitcast_fusion
  2.0 0.8 copy.13
  2.8 0.7 reshape_squeeze.8.coords_ref
  3.5 32.7 %shard_map.113.gathered_ref = bf16[32,128,128]{2,1,0:T(8,128)(2,1)} custom-call(bf16[128,128]{1,0:T(8,128)(2,1)} %bitcast.32), custom_call_target="tpu_custom_call" | custom-call | tf_op jit(solution)/shard_map/pallas_call | solution.py:131
  36.2 4.1 %shard_map.114.src_ref = bf16[16,128,128]{2,1,0:T(8,128)(2,1)} custom-call(s32[256]{0:T(256)} %reshape_squeeze.8.coords_ref, s32[1]{0:T(128)} %bitcast.26.count_ref, bf16[128,128,128]{2,1,0:T(8,128)(2,1)} %bitcast.28, bf16[32,128,128]{2,1,0:T(8,128)(2,1)} %shard_map.113.gathered_ref), custom_call_target="tpu_custom_call" | custom-call | tf_op jit(solution)/shard_map/pallas_call | solution.py:245
  40.3 28.3 %shard_map.115 = bf16[16,128,128]{2,1,0:T(8,128)(2,1)} custom-call(bf16[16,128,128]{2,1,0:T(8,128)(2,1)} %shard_map.114.src_ref), custom_call_target="tpu_custom_call" | custom-call | tf_op jit(solution)/shard_map/pallas_call | solution.py:146
  68.5 1.1 convert_reduce_fusion.1
  69.7 0.0 copy-done.3
  69.7 0.0 copy-done.4
  69.7 0.0 copy-done.5
  69.7 0.0 copy-done.6
  69.7 0.2 fusion.2
  69.9 0.0 copy-start.2
  69.9 0.0 copy-done
  69.9 0.8 convolution_convert_fusion
  70.7 36.0 %shard_map.116.gathered_ref = bf16[32,172,128]{2,1,0:T(8,128)(2,1)} custom-call(bf16[172,128]{1,0:T(8,128)(2,1)} %bitcast.30), custom_call_target="tpu_custom_call" | custom-call | tf_op jit(solution)/shard_map/pallas_call | solution.py:131
  106.7 4.7 %shard_map.117.src_ref = bf16[16,172,128]{2,1,0:T(8,128)(2,1)} custom-call(s32[256]{0:T(256)} %reshape_squeeze.8.coords_ref, s32[1]{0:T(128)} %bitcast.27.count_ref, bf16[128,128,128]{2,1,0:T(8,128)(2,1)} %bitcast.29, bf16[32,172,128]{2,1,0:T(8,128)(2,1)} %shard_map.116.gathered_ref), custom_call_target="tpu_custom_call" | custom-call | tf_op jit(solution)/shard_map/pallas_call | solution.py:245
  111.4 0.0 copy-done.2
  111.4 35.8 %shard_map.118 = bf16[16,172,128]{2,1,0:T(8,128)(2,1)} custom-call(bf16[16,172,128]{2,1,0:T(8,128)(2,1)} %shard_map.117.src_ref), custom_call_target="tpu_custom_call" | custom-call | tf_op jit(solution)/shard_map/pallas_call | solution.py:146
  147.2 1.2 convert_reduce_fusion
  148.5 0.0 copy-done.7
  148.5 0.1 fusion.4
  148.6 0.7 copy.14
  (7 shorter events, 0.0 us)
Async XLA Ops:
  0.6 69.3 %copy-start = (bf16[256,172]{0,1:T(8,128)(2,1)S(1)}, bf16[256,172]{0,1:T(8,128)(2,1)}, u32[]{:S(2)}) copy-start(bf16[256,172]{0,1:T(8,128)(2,1)} %param.18) | copy-start | bytes 264196
  40.3 29.4 %copy-start.3 = (bf16[1,1,128,128]{3,2,1,0:T(8,128)(2,1)S(1)}, bf16[1,1,128,128]{3,2,1,0:T(8,128)(2,1)}, u32[]{:S(2)}) copy-start(bf16[1,1,128,128]{3,2,1,0:T(8,128)(2,1)} %param.10) | copy-start | bytes 98308
  40.3 29.4 %copy-start.4 = (bf16[128,256]{1,0:T(8,128)(2,1)S(1)}, bf16[128,256]{1,0:T(8,128)(2,1)}, u32[]{:S(2)}) copy-start(bf16[128,256]{1,0:T(8,128)(2,1)} %param.16) | copy-start | bytes 196612
  40.3 29.4 %copy-start.5 = (bf16[1,1,128,256]{3,2,1,0:T(8,128)(2,1)S(1)}, bf16[1,1,128,256]{3,2,1,0:T(8,128)(2,1)}, u32[]{:S(2)}) copy-start(bf16[1,1,128,256]{3,2,1,0:T(8,128)(2,1)} %param.15) | copy-start | bytes 196612
  40.3 29.4 %copy-start.6 = (f32[256]{0:T(256)S(1)}, f32[256]{0:T(256)}, u32[]{:S(2)}) copy-start(f32[256]{0:T(256)} %param.17) | copy-start | bytes 3076
  69.9 41.5 %copy-start.2 = (bf16[128,256]{1,0:T(8,128)(2,1)}, bf16[128,256]{1,0:T(8,128)(2,1)S(1)}, u32[]{:S(2)}) copy-start(bf16[128,256]{1,0:T(8,128)(2,1)S(1)} %fusion.2) | copy-start | bytes 196612
  111.4 37.1 %copy-start.1 = (bf16[128,172]{0,1:T(8,128)(2,1)S(1)}, bf16[128,172]{0,1:T(8,128)(2,1)}, u32[]{:S(2)}) copy-start(bf16[128,172]{0,1:T(8,128)(2,1)} %convolution_convert_fusion) | copy-start | bytes 132100
  111.4 37.1 %copy-start.7 = (f32[172]{0:T(256)S(1)}, f32[172]{0:T(256)}, u32[]{:S(2)}) copy-start(f32[172]{0:T(256)} %param.19) | copy-start | bytes 2068

commit v7 on v6

--- a/solution.py
+++ b/solution.py
@@ -180,72 +180,72 @@
     return arrived.astype(jnp.float32).sum(axis=0)
 
 
-def products_kernel(group, flipped, coords_ref, count_ref, tiles_ref, gathered_ref, out_ref, total_ref):
-    step = pl.program_id(0)
-
-    @pl.when(step == 0)
-    def _():
-        total_ref[...] = jnp.zeros_like(total_ref)
-
+def products_kernel(
+    flipped, coords_ref, count_ref, tiles_ref, gathered_ref, out_ref, order_ref, bounds_ref, cursor_ref
+):
+    blocks = out_ref.shape[0]
     live = count_ref[0]
-
-    def one_tile(j, carry):
-        slot = step * group + j
-
-        @pl.when(slot < live)
-        def _():
-            target = coords_ref[2 * slot]
-            source = coords_ref[2 * slot + 1]
-            if flipped:
-                product = lax.dot_general(
-                    gathered_ref[source],
-                    tiles_ref[j],
-                    (((1,), (1,)), ((), ())),
-                    preferred_element_type=jnp.float32,
-                )
-            else:
-                product = jnp.dot(
-                    tiles_ref[j], gathered_ref[source], preferred_element_type=jnp.float32
-                )
-            total_ref[target] += product
-
-        return carry
-
-    @pl.when(step * group < live)
-    def _():
-        lax.fori_loop(0, group, one_tile, 0, unroll=True)
-
-    @pl.when(step == pl.num_programs(0) - 1)
-    def _():
-        out_ref[...] = total_ref[...].astype(out_ref.dtype)
-
-
-def tile_products(gathered, tiles, coords, live_total, flipped=False, group=16):
+    for target in range(blocks + 1):
+        bounds_ref[target] = 0
+
+    def count(slot, carry):
+        target = coords_ref[2 * slot]
+        bounds_ref[target + 1] = bounds_ref[target + 1] + 1
+        return carry
+
+    lax.fori_loop(0, live, count, 0)
+    for target in range(blocks):
+        bounds_ref[target + 1] = bounds_ref[target + 1] + bounds_ref[target]
+        cursor_ref[target] = bounds_ref[target]
+
+    def place(slot, carry):
+        target = coords_ref[2 * slot]
+        position = cursor_ref[target]
+        order_ref[position] = slot
+        cursor_ref[target] = position + 1
+        return carry
+
+    lax.fori_loop(0, live, place, 0)
+
+    def product(slot, total):
+        source = coords_ref[2 * slot + 1]
+        if flipped:
+            return total + lax.dot_general(
+                gathered_ref[source],
+                tiles_ref[slot],
+                (((1,), (1,)), ((), ())),
+                preferred_element_type=jnp.float32,
+            )
+        return total + jnp.dot(
+            tiles_ref[slot], gathered_ref[source], preferred_element_type=jnp.float32
+        )
+
+    for target in range(blocks):
+        total = lax.fori_loop(
+            bounds_ref[target],
+            bounds_ref[target + 1],
+            lambda position, total: product(order_ref[position], total),
+            jnp.zeros(out_ref.shape[1:], jnp.float32),
+        )
+        out_ref[target] = total.astype(out_ref.dtype)
+
+
+def tile_products(gathered, tiles, coords, live_total, flipped=False):
     row_blocks = lax.axis_size("col")
-    slots, size, _ = tiles.shape
+    slots = tiles.shape[0]
     block_shape = gathered.shape[1:]
-    steps = slots // group
-
-    def tile_map(step, coords_ref, count_ref):
-        return (jnp.minimum(step, (count_ref[0] - 1) // group), 0, 0)
-
-    def whole(step, coords_ref, count_ref):
-        return (0, 0, 0)
-
-    grid_spec = pltpu.PrefetchScalarGridSpec(
-        num_scalar_prefetch=2,
-        grid=(steps,),
-        in_specs=[
-            pl.BlockSpec((group, size, size), tile_map),
-            pl.BlockSpec(gathered.shape, whole),
+    vmem = pl.BlockSpec(memory_space=pltpu.VMEM)
+    smem = pl.BlockSpec(memory_space=pltpu.SMEM)
+    return pl.pallas_call(
+        functools.partial(products_kernel, flipped),
+        in_specs=[smem, smem, vmem, vmem],
+        out_specs=vmem,
+        out_shape=jax.ShapeDtypeStruct((row_blocks, *block_shape), jnp.bfloat16),
+        scratch_shapes=[
+            pltpu.SMEM((slots,), jnp.int32),
+            pltpu.SMEM((row_blocks + 1,), jnp.int32),
+            pltpu.SMEM((row_blocks,), jnp.int32),
         ],
-        out_specs=pl.BlockSpec((row_blocks, *block_shape), whole),
-        scratch_shapes=[pltpu.VMEM((row_blocks, *block_shape), jnp.float32)],
-    )
-    return pl.pallas_call(
-        functools.partial(products_kernel, group, flipped),
-        grid_spec=grid_spec,
-        out_shape=jax.ShapeDtypeStruct((row_blocks, *block_shape), jnp.bfloat16),
     )(coords.reshape(-1), live_total.reshape(1), tiles, gathered)
 
 

time: 152 us -> 159 us (1.046); the launches traced: 149 us -> 158 us
  Pallas kernels: 142 us -> 150 us
    pallas_call x2, Pallas kernels: 64.1 us -> 74.6 us  [exchange(): pl.pallas_call(functools.partial(exchange_kernel, axis, other_axis, n, sp...]
where the time goes in v7:
time: 159 us; the launch traced here: 158 us
  Pallas kernels  150 us (94%)
  other arithmetic  3.09 us (2%)
  local copies, waits for them, and re-layouts  2.27 us (1%)
    pallas_call x2, Pallas kernels, exchange(): pl.pallas_call(functools.partial(exchange_kernel, axis, other_axis, n, sp...  74.6 us
    pallas_call x2, Pallas kernels, gather(): pl.pallas_call(functools.partial(gather_kernel, n), out_shape=jax.ShapeDt...  67.2 us
    pallas_call x2, Pallas kernels, tile_products(): pl.pallas_call(functools.partial(products_kernel, flipped), in_specs=[sme...  8.59 us

profile of v7, /device:TPU:1, one launch (start us, length us, event | category | flops | bytes accessed | tf_op | source)
XLA Modules:
  0.0 158.1 jit_solution(9536115893132049152)
XLA Ops:
  0.6 0.0 copy-start
  1.3 0.7 compare_bitcast_fusion
  2.0 0.8 copy.13
  2.8 0.7 reshape_squeeze.8.coords_ref
  3.5 32.7 %shard_map.113.gathered_ref = bf16[32,128,128]{2,1,0:T(8,128)(2,1)} custom-call(bf16[128,128]{1,0:T(8,128)(2,1)} %bitcast.32), custom_call_target="tpu_custom_call" | custom-call | tf_op jit(solution)/shard_map/pallas_call | solution.py:131
  36.2 4.1 %shard_map.114.src_ref = bf16[16,128,128]{2,1,0:T(8,128)(2,1)} custom-call(s32[256]{0:T(256)} %reshape_squeeze.8.coords_ref, s32[1]{0:T(128)} %bitcast.26.count_ref, bf16[128,128,128]{2,1,0:T(8,128)(2,1)} %bitcast.28, bf16[32,128,128]{2,1,0:T(8,128)(2,1)} %shard_map.113.gathered_ref), custom_call_target="tpu_custom_call" | custom-call | tf_op jit(solution)/shard_map/pallas_call | solution.py:239
  40.3 33.7 %shard_map.115 = bf16[16,128,128]{2,1,0:T(8,128)(2,1)} custom-call(bf16[16,128,128]{2,1,0:T(8,128)(2,1)} %shard_map.114.src_ref), custom_call_target="tpu_custom_call" | custom-call | tf_op jit(solution)/shard_map/pallas_call | solution.py:146
  74.0 1.1 convert_reduce_fusion.1
  75.1 0.0 copy-done.3
  75.2 0.0 copy-done.4
  75.2 0.0 copy-done.5
  75.2 0.0 copy-done.6
  75.2 0.2 fusion.2
  75.4 0.0 copy-start.2
  75.4 0.0 copy-done
  75.4 0.8 convolution_convert_fusion
  76.2 34.5 %shard_map.116.gathered_ref = bf16[32,172,128]{2,1,0:T(8,128)(2,1)} custom-call(bf16[172,128]{1,0:T(8,128)(2,1)} %bitcast.30), custom_call_target="tpu_custom_call" | custom-call | tf_op jit(solution)/shard_map/pallas_call | solution.py:131
  110.7 4.5 %shard_map.117.src_ref = bf16[16,172,128]{2,1,0:T(8,128)(2,1)} custom-call(s32[256]{0:T(256)} %reshape_squeeze.8.coords_ref, s32[1]{0:T(128)} %bitcast.27.count_ref, bf16[128,128,128]{2,1,0:T(8,128)(2,1)} %bitcast.29, bf16[32,172,128]{2,1,0:T(8,128)(2,1)} %shard_map.116.gathered_ref), custom_call_target="tpu_custom_call" | custom-call | tf_op jit(solution)/shard_map/pallas_call | solution.py:239
  115.2 0.0 copy-done.2
  115.2 40.8 %shard_map.118 = bf16[16,172,128]{2,1,0:T(8,128)(2,1)} custom-call(bf16[16,172,128]{2,1,0:T(8,128)(2,1)} %shard_map.117.src_ref), custom_call_target="tpu_custom_call" | custom-call | tf_op jit(solution)/shard_map/pallas_call | solution.py:146
  156.0 1.2 convert_reduce_fusion
  157.3 0.0 copy-done.1
  157.3 0.1 fusion.4
  157.4 0.7 copy.14
  (7 shorter events, 0.0 us)
Async XLA Ops:
  0.6 74.7 %copy-start = (bf16[256,172]{0,1:T(8,128)(2,1)S(1)}, bf16[256,172]{0,1:T(8,128)(2,1)}, u32[]{:S(2)}) copy-start(bf16[256,172]{0,1:T(8,128)(2,1)} %param.18) | copy-start | bytes 264196
  40.3 34.9 %copy-start.3 = (bf16[1,1,128,128]{3,2,1,0:T(8,128)(2,1)S(1)}, bf16[1,1,128,128]{3,2,1,0:T(8,128)(2,1)}, u32[]{:S(2)}) copy-start(bf16[1,1,128,128]{3,2,1,0:T(8,128)(2,1)} %param.10) | copy-start | bytes 98308
  40.3 34.9 %copy-start.4 = (bf16[128,256]{1,0:T(8,128)(2,1)S(1)}, bf16[128,256]{1,0:T(8,128)(2,1)}, u32[]{:S(2)}) copy-start(bf16[128,256]{1,0:T(8,128)(2,1)} %param.16) | copy-start | bytes 196612
  40.3 34.9 %copy-start.5 = (bf16[1,1,128,256]{3,2,1,0:T(8,128)(2,1)S(1)}, bf16[1,1,128,256]{3,2,1,0:T(8,128)(2,1)}, u32[]{:S(2)}) copy-start(bf16[1,1,128,256]{3,2,1,0:T(8,128)(2,1)} %param.15) | copy-start | bytes 196612
  40.3 34.9 %copy-start.6 = (f32[256]{0:T(256)S(1)}, f32[256]{0:T(256)}, u32[]{:S(2)}) copy-start(f32[256]{0:T(256)} %param.17) | copy-start | bytes 3076
  75.4 39.8 %copy-start.2 = (bf16[128,256]{1,0:T(8,128)(2,1)}, bf16[128,256]{1,0:T(8,128)(2,1)S(1)}, u32[]{:S(2)}) copy-start(bf16[128,256]{1,0:T(8,128)(2,1)S(1)} %fusion.2) | copy-start | bytes 196612
  115.2 42.1 %copy-start.1 = (bf16[128,172]{0,1:T(8,128)(2,1)S(1)}, bf16[128,172]{0,1:T(8,128)(2,1)}, u32[]{:S(2)}) copy-start(bf16[128,172]{0,1:T(8,128)(2,1)} %convolution_convert_fusion) | copy-start | bytes 132100
  115.2 42.1 %copy-start.7 = (f32[172]{0:T(256)S(1)}, f32[172]{0:T(256)}, u32[]{:S(2)}) copy-start(f32[172]{0:T(256)} %param.19) | copy-start | bytes 2068

commit v8 on v7

--- a/solution.py
+++ b/solution.py
@@ -181,7 +181,7 @@
 
 
 def products_kernel(
-    flipped, coords_ref, count_ref, tiles_ref, gathered_ref, out_ref, order_ref, bounds_ref, cursor_ref
+    flipped, pack, coords_ref, count_ref, tiles_ref, gathered_ref, out_ref, order_ref, bounds_ref, cursor_ref
 ):
     blocks = out_ref.shape[0]
     live = count_ref[0]
@@ -207,37 +207,45 @@
 
     lax.fori_loop(0, live, place, 0)
 
-    def product(slot, total):
-        source = coords_ref[2 * slot + 1]
+    def product(first, end, total):
+        tiles, sources = [], []
+        for offset in range(pack):
+            slot = order_ref[jnp.minimum(first + offset, end - 1)]
+            tile = tiles_ref[slot]
+            tiles.append(jnp.where(first + offset < end, tile, jnp.zeros_like(tile)))
+            sources.append(gathered_ref[coords_ref[2 * slot + 1]])
         if flipped:
             return total + lax.dot_general(
-                gathered_ref[source],
-                tiles_ref[slot],
+                jnp.concatenate(sources, axis=1),
+                jnp.concatenate(tiles, axis=1),
                 (((1,), (1,)), ((), ())),
                 preferred_element_type=jnp.float32,
             )
         return total + jnp.dot(
-            tiles_ref[slot], gathered_ref[source], preferred_element_type=jnp.float32
+            jnp.concatenate(tiles, axis=1),
+            jnp.concatenate(sources, axis=0),
+            preferred_element_type=jnp.float32,
         )
 
     for target in range(blocks):
+        first, end = bounds_ref[target], bounds_ref[target + 1]
         total = lax.fori_loop(
-            bounds_ref[target],
-            bounds_ref[target + 1],
-            lambda position, total: product(order_ref[position], total),
+            0,
+            (end - first + pack - 1) // pack,
+            lambda step, total: product(first + step * pack, end, total),
             jnp.zeros(out_ref.shape[1:], jnp.float32),
         )
         out_ref[target] = total.astype(out_ref.dtype)
 
 
-def tile_products(gathered, tiles, coords, live_total, flipped=False):
+def tile_products(gathered, tiles, coords, live_total, flipped=False, pack=4):
     row_blocks = lax.axis_size("col")
     slots = tiles.shape[0]
     block_shape = gathered.shape[1:]
     vmem = pl.BlockSpec(memory_space=pltpu.VMEM)
     smem = pl.BlockSpec(memory_space=pltpu.SMEM)
     return pl.pallas_call(
-        functools.partial(products_kernel, flipped),
+        functools.partial(products_kernel, flipped, pack),
         in_specs=[smem, smem, vmem, vmem],
         out_specs=vmem,
         out_shape=jax.ShapeDtypeStruct((row_blocks, *block_shape), jnp.bfloat16),

time: 159 us -> 137 us (0.86)
  Pallas kernels: 150 us -> 129 us
    pallas_call x2, Pallas kernels: 74.6 us -> 49.9 us  [exchange(): pl.pallas_call(functools.partial(exchange_kernel, axis, other_axis, n, sp...]
    pallas_call x2, Pallas kernels: 8.59 us -> 14.1 us  [tile_products(): pl.pallas_call(functools.partial(products_kernel, flipped, pack), in_spec...]
    pallas_call x2, Pallas kernels: 67.2 us -> 64.6 us  [gather(): pl.pallas_call(functools.partial(gather_kernel, n), out_shape=jax.ShapeDt...]
where the time goes in v8:
time: 137 us; the launch traced here: 136 us
  Pallas kernels  129 us (94%)
  other arithmetic  3.09 us (2%)
  local copies, waits for them, and re-layouts  2.27 us (2%)
  between operations  1.44 us (1%)
    pallas_call x2, Pallas kernels, gather(): pl.pallas_call(functools.partial(gather_kernel, n), out_shape=jax.ShapeDt...  64.6 us
    pallas_call x2, Pallas kernels, exchange(): pl.pallas_call(functools.partial(exchange_kernel, axis, other_axis, n, sp...  49.9 us
    pallas_call x2, Pallas kernels, tile_products(): pl.pallas_call(functools.partial(products_kernel, flipped, pack), in_spec...  14.1 us

profile of v8, /device:TPU:1, one launch (start us, length us, event | category | flops | bytes accessed | tf_op | source)
XLA Modules:
  0.0 136.4 jit_solution(12833565599533110633)
XLA Ops:
  0.6 0.0 copy-start
  1.3 0.7 compare_bitcast_fusion
  2.0 0.8 copy.13
  2.8 0.7 reshape_squeeze.8.coords_ref
  3.5 32.7 %shard_map.113.gathered_ref = bf16[32,128,128]{2,1,0:T(8,128)(2,1)} custom-call(bf16[128,128]{1,0:T(8,128)(2,1)} %bitcast.32), custom_call_target="tpu_custom_call" | custom-call | tf_op jit(solution)/shard_map/pallas_call | solution.py:131
  36.2 6.7 %shard_map.114.src_ref = bf16[16,128,128]{2,1,0:T(8,128)(2,1)} custom-call(s32[256]{0:T(256)} %reshape_squeeze.8.coords_ref, s32[1]{0:T(128)} %bitcast.26.count_ref, bf16[128,128,128]{2,1,0:T(8,128)(2,1)} %bitcast.28, bf16[32,128,128]{2,1,0:T(8,128)(2,1)} %shard_map.113.gathered_ref), custom_call_target="tpu_custom_call" | custom-call | tf_op jit(solution)/shard_map/pallas_call | solution.py:247
  42.9 23.0 %shard_map.115 = bf16[16,128,128]{2,1,0:T(8,128)(2,1)} custom-call(bf16[16,128,128]{2,1,0:T(8,128)(2,1)} %shard_map.114.src_ref), custom_call_target="tpu_custom_call" | custom-call | tf_op jit(solution)/shard_map/pallas_call | solution.py:146
  65.9 1.1 convert_reduce_fusion.1
  67.0 0.0 copy-done.3
  67.0 0.0 copy-done.4
  67.1 0.0 copy-done.5
  67.1 0.0 copy-done.6
  67.1 0.2 fusion.2
  67.2 0.0 copy-start.2
  67.2 0.0 copy-done
  67.3 0.8 convolution_convert_fusion
  68.1 31.9 %shard_map.116.gathered_ref = bf16[32,172,128]{2,1,0:T(8,128)(2,1)} custom-call(bf16[172,128]{1,0:T(8,128)(2,1)} %bitcast.30), custom_call_target="tpu_custom_call" | custom-call | tf_op jit(solution)/shard_map/pallas_call | solution.py:131
  100.0 7.4 %shard_map.117.src_ref = bf16[16,172,128]{2,1,0:T(8,128)(2,1)} custom-call(s32[256]{0:T(256)} %reshape_squeeze.8.coords_ref, s32[1]{0:T(128)} %bitcast.27.count_ref, bf16[128,128,128]{2,1,0:T(8,128)(2,1)} %bitcast.29, bf16[32,172,128]{2,1,0:T(8,128)(2,1)} %shard_map.116.gathered_ref), custom_call_target="tpu_custom_call" | custom-call | tf_op jit(solution)/shard_map/pallas_call | solution.py:247
  107.4 0.0 copy-done.2
  107.4 26.9 %shard_map.118 = bf16[16,172,128]{2,1,0:T(8,128)(2,1)} custom-call(bf16[16,172,128]{2,1,0:T(8,128)(2,1)} %shard_map.117.src_ref), custom_call_target="tpu_custom_call" | custom-call | tf_op jit(solution)/shard_map/pallas_call | solution.py:146
  134.4 1.2 convert_reduce_fusion
  135.6 0.0 copy-done.1
  135.6 0.1 fusion.4
  135.7 0.7 copy.14
  (7 shorter events, 0.0 us)
Async XLA Ops:
  0.6 66.6 %copy-start = (bf16[256,172]{0,1:T(8,128)(2,1)S(1)}, bf16[256,172]{0,1:T(8,128)(2,1)}, u32[]{:S(2)}) copy-start(bf16[256,172]{0,1:T(8,128)(2,1)} %param.18) | copy-start | bytes 264196
  42.9 24.1 %copy-start.3 = (bf16[1,1,128,128]{3,2,1,0:T(8,128)(2,1)S(1)}, bf16[1,1,128,128]{3,2,1,0:T(8,128)(2,1)}, u32[]{:S(2)}) copy-start(bf16[1,1,128,128]{3,2,1,0:T(8,128)(2,1)} %param.10) | copy-start | bytes 98308
  42.9 24.1 %copy-start.4 = (bf16[128,256]{1,0:T(8,128)(2,1)S(1)}, bf16[128,256]{1,0:T(8,128)(2,1)}, u32[]{:S(2)}) copy-start(bf16[128,256]{1,0:T(8,128)(2,1)} %param.16) | copy-start | bytes 196612
  42.9 24.2 %copy-start.5 = (bf16[1,1,128,256]{3,2,1,0:T(8,128)(2,1)S(1)}, bf16[1,1,128,256]{3,2,1,0:T(8,128)(2,1)}, u32[]{:S(2)}) copy-start(bf16[1,1,128,256]{3,2,1,0:T(8,128)(2,1)} %param.15) | copy-start | bytes 196612
  42.9 24.2 %copy-start.6 = (f32[256]{0:T(256)S(1)}, f32[256]{0:T(256)}, u32[]{:S(2)}) copy-start(f32[256]{0:T(256)} %param.17) | copy-start | bytes 3076
  67.2 40.2 %copy-start.2 = (bf16[128,256]{1,0:T(8,128)(2,1)}, bf16[128,256]{1,0:T(8,128)(2,1)S(1)}, u32[]{:S(2)}) copy-start(bf16[128,256]{1,0:T(8,128)(2,1)S(1)} %fusion.2) | copy-start | bytes 196612
  107.4 28.1 %copy-start.1 = (bf16[128,172]{0,1:T(8,128)(2,1)S(1)}, bf16[128,172]{0,1:T(8,128)(2,1)}, u32[]{:S(2)}) copy-start(bf16[128,172]{0,1:T(8,128)(2,1)} %convolution_convert_fusion) | copy-start | bytes 132100
  107.4 28.1 %copy-start.7 = (f32[172]{0:T(256)S(1)}, f32[172]{0:T(256)}, u32[]{:S(2)}) copy-start(f32[172]{0:T(256)} %param.19) | copy-start | bytes 2068

commit v9 on v8

--- a/solution.py
+++ b/solution.py
@@ -238,7 +238,7 @@
         out_ref[target] = total.astype(out_ref.dtype)
 
 
-def tile_products(gathered, tiles, coords, live_total, flipped=False, pack=4):
+def tile_products(gathered, tiles, coords, live_total, flipped=False, pack=8):
     row_blocks = lax.axis_size("col")
     slots = tiles.shape[0]
     block_shape = gathered.shape[1:]

time: 137 us -> 135 us (0.985)
  the two profiles are of different devices: /device:TPU:1 before, /device:TPU:8 now
where the time goes in v9:
time: 135 us
  Pallas kernels  127 us (94%)
  other arithmetic  3.09 us (2%)
  local copies, waits for them, and re-layouts  2.27 us (2%)
  between operations  1.44 us (1%)
    pallas_call x2, Pallas kernels, gather(): pl.pallas_call(functools.partial(gather_kernel, n), out_shape=jax.ShapeDt...  58.3 us
    pallas_call x2, Pallas kernels, exchange(): pl.pallas_call(functools.partial(exchange_kernel, axis, other_axis, n, sp...  50.4 us
    pallas_call x2, Pallas kernels, tile_products(): pl.pallas_call(functools.partial(products_kernel, flipped, pack), in_spec...  18.2 us

profile of v9, /device:TPU:8, one launch (start us, length us, event | category | flops | bytes accessed | tf_op | source)
XLA Modules:
  0.0 134.6 jit_solution(15336647250481469449)
XLA Ops:
  0.6 0.0 copy-start
  1.3 0.7 compare_bitcast_fusion
  2.0 0.8 copy.13
  2.8 0.7 reshape_squeeze.8.coords_ref
  3.5 30.5 %shard_map.113.gathered_ref = bf16[32,128,128]{2,1,0:T(8,128)(2,1)} custom-call(bf16[128,128]{1,0:T(8,128)(2,1)} %bitcast.32), custom_call_target="tpu_custom_call" | custom-call | tf_op jit(solution)/shard_map/pallas_call | solution.py:131
  34.0 8.6 %shard_map.114.src_ref = bf16[16,128,128]{2,1,0:T(8,128)(2,1)} custom-call(s32[256]{0:T(256)} %reshape_squeeze.8.coords_ref, s32[1]{0:T(128)} %bitcast.26.count_ref, bf16[128,128,128]{2,1,0:T(8,128)(2,1)} %bitcast.28, bf16[32,128,128]{2,1,0:T(8,128)(2,1)} %shard_map.113.gathered_ref), custom_call_target="tpu_custom_call" | custom-call | tf_op jit(solution)/shard_map/pallas_call | solution.py:247
  42.6 23.1 %shard_map.115 = bf16[16,128,128]{2,1,0:T(8,128)(2,1)} custom-call(bf16[16,128,128]{2,1,0:T(8,128)(2,1)} %shard_map.114.src_ref), custom_call_target="tpu_custom_call" | custom-call | tf_op jit(solution)/shard_map/pallas_call | solution.py:146
  65.7 1.1 convert_reduce_fusion.1
  66.9 0.0 copy-done.3
  66.9 0.0 copy-done.4
  66.9 0.0 copy-done.5
  66.9 0.0 copy-done.6
  66.9 0.2 fusion.2
  67.1 0.0 copy-start.2
  67.1 0.0 copy-done
  67.1 0.8 convolution_convert_fusion
  67.9 27.8 %shard_map.116.gathered_ref = bf16[32,172,128]{2,1,0:T(8,128)(2,1)} custom-call(bf16[172,128]{1,0:T(8,128)(2,1)} %bitcast.30), custom_call_target="tpu_custom_call" | custom-call | tf_op jit(solution)/shard_map/pallas_call | solution.py:131
  95.7 9.5 %shard_map.117.src_ref = bf16[16,172,128]{2,1,0:T(8,128)(2,1)} custom-call(s32[256]{0:T(256)} %reshape_squeeze.8.coords_ref, s32[1]{0:T(128)} %bitcast.27.count_ref, bf16[128,128,128]{2,1,0:T(8,128)(2,1)} %bitcast.29, bf16[32,172,128]{2,1,0:T(8,128)(2,1)} %shard_map.116.gathered_ref), custom_call_target="tpu_custom_call" | custom-call | tf_op jit(solution)/shard_map/pallas_call | solution.py:247
  105.2 0.0 copy-done.2
  105.2 27.4 %shard_map.118 = bf16[16,172,128]{2,1,0:T(8,128)(2,1)} custom-call(bf16[16,172,128]{2,1,0:T(8,128)(2,1)} %shard_map.117.src_ref), custom_call_target="tpu_custom_call" | custom-call | tf_op jit(solution)/shard_map/pallas_call | solution.py:146
  132.6 1.2 convert_reduce_fusion
  133.8 0.0 copy-done.7
  133.8 0.1 fusion.4
  133.9 0.7 copy.14
  (7 shorter events, 0.0 us)
Async XLA Ops:
  0.6 66.4 %copy-start = (bf16[256,172]{0,1:T(8,128)(2,1)S(1)}, bf16[256,172]{0,1:T(8,128)(2,1)}, u32[]{:S(2)}) copy-start(bf16[256,172]{0,1:T(8,128)(2,1)} %param.18) | copy-start | bytes 264196
  42.6 24.2 %copy-start.3 = (bf16[1,1,128,128]{3,2,1,0:T(8,128)(2,1)S(1)}, bf16[1,1,128,128]{3,2,1,0:T(8,128)(2,1)}, u32[]{:S(2)}) copy-start(bf16[1,1,128,128]{3,2,1,0:T(8,128)(2,1)} %param.10) | copy-start | bytes 98308
  42.6 24.2 %copy-start.4 = (bf16[128,256]{1,0:T(8,128)(2,1)S(1)}, bf16[128,256]{1,0:T(8,128)(2,1)}, u32[]{:S(2)}) copy-start(bf16[128,256]{1,0:T(8,128)(2,1)} %param.16) | copy-start | bytes 196612
  42.6 24.3 %copy-start.5 = (bf16[1,1,128,256]{3,2,1,0:T(8,128)(2,1)S(1)}, bf16[1,1,128,256]{3,2,1,0:T(8,128)(2,1)}, u32[]{:S(2)}) copy-start(bf16[1,1,128,256]{3,2,1,0:T(8,128)(2,1)} %param.15) | copy-start | bytes 196612
  42.6 24.3 %copy-start.6 = (f32[256]{0:T(256)S(1)}, f32[256]{0:T(256)}, u32[]{:S(2)}) copy-start(f32[256]{0:T(256)} %param.17) | copy-start | bytes 3076
  67.1 38.1 %copy-start.2 = (bf16[128,256]{1,0:T(8,128)(2,1)}, bf16[128,256]{1,0:T(8,128)(2,1)S(1)}, u32[]{:S(2)}) copy-start(bf16[128,256]{1,0:T(8,128)(2,1)S(1)} %fusion.2) | copy-start | bytes 196612
  105.2 28.6 %copy-start.1 = (bf16[128,172]{0,1:T(8,128)(2,1)S(1)}, bf16[128,172]{0,1:T(8,128)(2,1)}, u32[]{:S(2)}) copy-start(bf16[128,172]{0,1:T(8,128)(2,1)} %convolution_convert_fusion) | copy-start | bytes 132100
  105.2 28.6 %copy-start.7 = (f32[172]{0:T(256)S(1)}, f32[172]{0:T(256)}, u32[]{:S(2)}) copy-start(f32[172]{0:T(256)} %param.19) | copy-start | bytes 2068

commit v10 on v9

--- a/solution.py
+++ b/solution.py
@@ -238,7 +238,7 @@
         out_ref[target] = total.astype(out_ref.dtype)
 
 
-def tile_products(gathered, tiles, coords, live_total, flipped=False, pack=8):
+def tile_products(gathered, tiles, coords, live_total, flipped=False, pack=16):
     row_blocks = lax.axis_size("col")
     slots = tiles.shape[0]
     block_shape = gathered.shape[1:]

time: 135 us -> 136 us (level)
  the two profiles are of different devices: /device:TPU:8 before, /device:TPU:1 now
where the time goes in v10:
time: 136 us; the launch traced here: 135 us
  Pallas kernels  127 us (93%)
  other arithmetic  3.09 us (2%)
  local copies, waits for them, and re-layouts  2.27 us (2%)
  between operations  1.44 us (1%)
    pallas_call x2, Pallas kernels, gather(): pl.pallas_call(functools.partial(gather_kernel, n), out_shape=jax.ShapeDt...  64.2 us
    pallas_call x2, Pallas kernels, exchange(): pl.pallas_call(functools.partial(exchange_kernel, axis, other_axis, n, sp...  42.6 us
    pallas_call x2, Pallas kernels, tile_products(): pl.pallas_call(functools.partial(products_kernel, flipped, pack), in_spec...  20.4 us

profile of v10, /device:TPU:1, one launch (start us, length us, event | category | flops | bytes accessed | tf_op | source)
XLA Modules:
  0.0 135.0 jit_solution(11003781976592753789)
XLA Ops:
  0.6 0.0 copy-start
  1.3 0.7 compare_bitcast_fusion
  2.0 0.8 copy.13
  2.8 0.7 reshape_squeeze.8.coords_ref
  3.5 32.7 %shard_map.113.gathered_ref = bf16[32,128,128]{2,1,0:T(8,128)(2,1)} custom-call(bf16[128,128]{1,0:T(8,128)(2,1)} %bitcast.32), custom_call_target="tpu_custom_call" | custom-call | tf_op jit(solution)/shard_map/pallas_call | solution.py:131
  36.2 9.6 %shard_map.114.src_ref = bf16[16,128,128]{2,1,0:T(8,128)(2,1)} custom-call(s32[256]{0:T(256)} %reshape_squeeze.8.coords_ref, s32[1]{0:T(128)} %bitcast.26.count_ref, bf16[128,128,128]{2,1,0:T(8,128)(2,1)} %bitcast.28, bf16[32,128,128]{2,1,0:T(8,128)(2,1)} %shard_map.113.gathered_ref), custom_call_target="tpu_custom_call" | custom-call | tf_op jit(solution)/shard_map/pallas_call | solution.py:247
  45.8 20.0 %shard_map.115 = bf16[16,128,128]{2,1,0:T(8,128)(2,1)} custom-call(bf16[16,128,128]{2,1,0:T(8,128)(2,1)} %shard_map.114.src_ref), custom_call_target="tpu_custom_call" | custom-call | tf_op jit(solution)/shard_map/pallas_call | solution.py:146
  65.8 1.1 convert_reduce_fusion.1
  66.9 0.0 copy-done.3
  66.9 0.0 copy-done.4
  66.9 0.0 copy-done.5
  66.9 0.0 copy-done.6
  67.0 0.2 fusion.2
  67.1 0.0 copy-start.2
  67.1 0.0 copy-done
  67.1 0.8 convolution_convert_fusion
  67.9 31.6 %shard_map.116.gathered_ref = bf16[32,172,128]{2,1,0:T(8,128)(2,1)} custom-call(bf16[172,128]{1,0:T(8,128)(2,1)} %bitcast.30), custom_call_target="tpu_custom_call" | custom-call | tf_op jit(solution)/shard_map/pallas_call | solution.py:131
  99.5 10.8 %shard_map.117.src_ref = bf16[16,172,128]{2,1,0:T(8,128)(2,1)} custom-call(s32[256]{0:T(256)} %reshape_squeeze.8.coords_ref, s32[1]{0:T(128)} %bitcast.27.count_ref, bf16[128,128,128]{2,1,0:T(8,128)(2,1)} %bitcast.29, bf16[32,172,128]{2,1,0:T(8,128)(2,1)} %shard_map.116.gathered_ref), custom_call_target="tpu_custom_call" | custom-call | tf_op jit(solution)/shard_map/pallas_call | solution.py:247
  110.4 0.0 copy-done.2
  110.4 22.6 %shard_map.118 = bf16[16,172,128]{2,1,0:T(8,128)(2,1)} custom-call(bf16[16,172,128]{2,1,0:T(8,128)(2,1)} %shard_map.117.src_ref), custom_call_target="tpu_custom_call" | custom-call | tf_op jit(solution)/shard_map/pallas_call | solution.py:146
  132.9 1.2 convert_reduce_fusion
  134.1 0.0 copy-done.1
  134.2 0.1 fusion.4
  134.3 0.7 copy.14
  (7 shorter events, 0.0 us)
Async XLA Ops:
  0.6 66.5 %copy-start = (bf16[256,172]{0,1:T(8,128)(2,1)S(1)}, bf16[256,172]{0,1:T(8,128)(2,1)}, u32[]{:S(2)}) copy-start(bf16[256,172]{0,1:T(8,128)(2,1)} %param.18) | copy-start | bytes 264196
  45.7 21.2 %copy-start.3 = (bf16[1,1,128,128]{3,2,1,0:T(8,128)(2,1)S(1)}, bf16[1,1,128,128]{3,2,1,0:T(8,128)(2,1)}, u32[]{:S(2)}) copy-start(bf16[1,1,128,128]{3,2,1,0:T(8,128)(2,1)} %param.10) | copy-start | bytes 98308
  45.7 21.2 %copy-start.4 = (bf16[128,256]{1,0:T(8,128)(2,1)S(1)}, bf16[128,256]{1,0:T(8,128)(2,1)}, u32[]{:S(2)}) copy-start(bf16[128,256]{1,0:T(8,128)(2,1)} %param.16) | copy-start | bytes 196612
  45.7 21.2 %copy-start.5 = (bf16[1,1,128,256]{3,2,1,0:T(8,128)(2,1)S(1)}, bf16[1,1,128,256]{3,2,1,0:T(8,128)(2,1)}, u32[]{:S(2)}) copy-start(bf16[1,1,128,256]{3,2,1,0:T(8,128)(2,1)} %param.15) | copy-start | bytes 196612
  45.8 21.2 %copy-start.6 = (f32[256]{0:T(256)S(1)}, f32[256]{0:T(256)}, u32[]{:S(2)}) copy-start(f32[256]{0:T(256)} %param.17) | copy-start | bytes 3076
  67.1 43.2 %copy-start.2 = (bf16[128,256]{1,0:T(8,128)(2,1)}, bf16[128,256]{1,0:T(8,128)(2,1)S(1)}, u32[]{:S(2)}) copy-start(bf16[128,256]{1,0:T(8,128)(2,1)S(1)} %fusion.2) | copy-start | bytes 196612
  110.4 23.8 %copy-start.1 = (bf16[128,172]{0,1:T(8,128)(2,1)S(1)}, bf16[128,172]{0,1:T(8,128)(2,1)}, u32[]{:S(2)}) copy-start(bf16[128,172]{0,1:T(8,128)(2,1)} %convolution_convert_fusion) | copy-start | bytes 132100
  110.4 23.8 %copy-start.7 = (f32[172]{0:T(256)S(1)}, f32[172]{0:T(256)}, u32[]{:S(2)}) copy-start(f32[172]{0:T(256)} %param.19) | copy-start | bytes 2068

commit v11 on v9

--- a/solution.py
+++ b/solution.py
@@ -65,10 +65,26 @@
     lax.fori_loop(1, n, finish, 0)
 
 
-def gather_kernel(n, src_ref, out_ref, send_sem, pass_sem, recv_sem):
+def row_partners():
     me = lax.axis_index("row")
-    other = lax.axis_index("col")
-    twin = me + 1 - 2 * lax.rem(me, 2)
+    return me, lax.axis_index("col"), me + 1 - 2 * lax.rem(me, 2)
+
+
+def row_greet(barrier, n):
+    me, other, twin = row_partners()
+    pl.semaphore_signal(barrier, 1, device_id=(twin, other), device_id_type=MESH_ID)
+
+    def greet(step, carry):
+        peer = lax.rem(me + 2 * step, n)
+        pl.semaphore_signal(barrier, 1, device_id=(peer, other), device_id_type=MESH_ID)
+        return carry
+
+    lax.fori_loop(1, n // 2, greet, 0)
+    return n // 2
+
+
+def row_transfer(n, src_ref, out_ref, send_sem, pass_sem, recv_sem):
+    me, other, twin = row_partners()
     half = n // 2
 
     def copy(source, slot, sems, k):
@@ -87,23 +103,12 @@
     def far(step):
         return lax.rem(twin + 2 * step, n)
 
-    barrier = pltpu.get_barrier_semaphore()
-    pl.semaphore_signal(barrier, 1, device_id=(twin, other), device_id_type=MESH_ID)
-
-    def greet(step, carry):
-        pl.semaphore_signal(barrier, 1, device_id=(peer(step), other), device_id_type=MESH_ID)
-        return carry
-
-    lax.fori_loop(1, half, greet, 0)
-    pl.semaphore_wait(barrier, half)
-
     def send(step, carry):
         copy(src_ref, me, send_sem, peer(step)).start()
         return carry
 
     lax.fori_loop(1, half, send, 0)
     copy(src_ref, me, send_sem, twin).start()
-    out_ref[me] = src_ref[...]
 
     def relay(step, carry):
         k = peer(step)
@@ -123,6 +128,13 @@
     lax.fori_loop(1, half, finish, 0)
     copy(src_ref, me, send_sem, twin).wait_send()
     copy(src_ref, twin, send_sem, twin).wait_recv()
+
+
+def gather_kernel(n, src_ref, out_ref, send_sem, pass_sem, recv_sem):
+    barrier = pltpu.get_barrier_semaphore()
+    pl.semaphore_wait(barrier, row_greet(barrier, n))
+    out_ref[lax.axis_index("row")] = src_ref[...]
+    row_transfer(n, src_ref, out_ref, send_sem, pass_sem, recv_sem)
 
 
 def gather(block, tag):
@@ -136,6 +148,109 @@
         scratch_shapes=[pltpu.SemaphoreType.DMA((n,))] * 3,
         compiler_params=pltpu.CompilerParams(collective_id=tag, has_side_effects=True),
     )(block)
+
+
+def middle_kernel(
+    n_row,
+    n_col,
+    parts_ref,
+    features_ref,
+    weight_one_ref,
+    bias_one_ref,
+    mask_ref,
+    history_ref,
+    weight_two_ref,
+    pushed_ref,
+    out_ref,
+    landing_ref,
+    col_send,
+    col_recv,
+    send_sem,
+    pass_sem,
+    recv_sem,
+):
+    row = lax.axis_index("row")
+    me = lax.axis_index("col")
+
+    def col_copy(k, slot):
+        return pltpu.make_async_remote_copy(
+            src_ref=parts_ref.at[k],
+            dst_ref=landing_ref.at[slot],
+            send_sem=col_send.at[k],
+            recv_sem=col_recv.at[slot],
+            device_id=(row, k),
+            device_id_type=MESH_ID,
+        )
+
+    barrier = pltpu.get_barrier_semaphore()
+
+    def greet(step, carry):
+        k = lax.rem(me + step, n_col)
+        pl.semaphore_signal(barrier, 1, device_id=(row, k), device_id_type=MESH_ID)
+        return carry
+
+    lax.fori_loop(1, n_col, greet, 0)
+    expected = row_greet(barrier, n_row)
+    pl.semaphore_wait(barrier, n_col - 1 + expected)
+
+    def send(step, carry):
+        col_copy(lax.rem(me + step, n_col), me).start()
+        return carry
+
+    lax.fori_loop(1, n_col, send, 0)
+    landing_ref[me] = parts_ref[me]
+
+    def finish(step, carry):
+        col_copy(lax.rem(me + step, n_col), me).wait_send()
+        col_copy(me, lax.rem(me + n_col - step, n_col)).wait_recv()
+        return carry
+
+    lax.fori_loop(1, n_col, finish, 0)
+    total = features_ref[...].astype(jnp.float32)
+    for k in range(n_col):
+        total = total + landing_ref[k].astype(jnp.float32)
+    agg = total.astype(jnp.bfloat16)
+    pre = jnp.dot(agg, weight_one_ref[...], preferred_element_type=jnp.float32)
+    hidden = jnp.maximum(pre + bias_one_ref[...], 0.0).astype(jnp.bfloat16)
+    pushed = jnp.where(mask_ref[...] == 1, hidden, history_ref[...])
+    pushed_ref[...] = pushed
+    projected = lax.dot_general(
+        weight_two_ref[...], pushed, (((1,), (1,)), ((), ())), preferred_element_type=jnp.float32
+    )
+    out_ref[row] = projected.astype(out_ref.dtype)
+    row_transfer(n_row, out_ref.at[row], out_ref, send_sem, pass_sem, recv_sem)
+
+
+def middle(parts, features, weight_one, bias_one, mask, history, weight_two, tag):
+    n_row = lax.axis_size("row")
+    n_col = lax.axis_size("col")
+    classes = weight_two.shape[1]
+    nodes = features.shape[0]
+    vmem = pl.BlockSpec(memory_space=pltpu.VMEM)
+    return pl.pallas_call(
+        functools.partial(middle_kernel, n_row, n_col),
+        out_shape=(
+            jax.ShapeDtypeStruct(history.shape, history.dtype),
+            jax.ShapeDtypeStruct((n_row, classes, nodes), jnp.bfloat16),
+        ),
+        in_specs=[vmem] * 7,
+        out_specs=(vmem, vmem),
+        scratch_shapes=[
+            pltpu.VMEM(parts.shape, parts.dtype),
+            pltpu.SemaphoreType.DMA((n_col,)),
+            pltpu.SemaphoreType.DMA((n_col,)),
+        ]
+        + [pltpu.SemaphoreType.DMA((n_row,))] * 3,
+        compiler_params=pltpu.CompilerParams(collective_id=tag, has_side_effects=True),
+    )(
+        parts,
+        features,
+        weight_one,
+        bias_one.reshape(1, -1),
+        mask.reshape(-1, 1),
+        history,
+        weight_two.T,
+    )
 
 
 def exchange(block, axis, spread, tag):
@@ -274,17 +389,20 @@
     live_total = tile_count[0, 0]
     gathered_input = gather(features[0, 0], 0)
     summed_one = tile_products(gathered_input, tile_set, coord_set, live_total)
-    owned_one = exchange(summed_one, "col", True, 1)
-    owned_one = owned_one.astype(jnp.float32).sum(axis=0)
-    agg_one = (features[0, 0].astype(jnp.float32) + owned_one).astype(jnp.bfloat16)
-    pre_one = jnp.dot(agg_one, weight_one, preferred_element_type=jnp.float32) + bias_one
-    hidden = jax.nn.relu(pre_one).astype(jnp.bfloat16)
-    pushed = jnp.where(batch_mask[0, 0][:, None] == 1, hidden, history[0, 0])
-    projected = jnp.dot(pushed, weight_two, preferred_element_type=jnp.float32).astype(jnp.bfloat16)
-    gathered_proj = gather(projected.T, 2)
+    pushed, gathered_proj = middle(
+        summed_one,
+        features[0, 0],
+        weight_one,
+        bias_one,
+        batch_mask[0, 0],
+        history[0, 0],
+        weight_two,
+        1,
+    )
     summed_two = tile_products(gathered_proj, tile_set, coord_set, live_total, True)
-    owned_two = exchange(summed_two, "col", True, 3).astype(jnp.float32).sum(axis=0).T
-    scores = projected.astype(jnp.float32) + owned_two + bias_two
+    owned_two = exchange(summed_two, "col", True, 3).astype(jnp.float32).sum(axis=0)
+    own_block = gathered_proj[lax.axis_index("row")].astype(jnp.float32)
+    scores = (own_block + owned_two).T + bias_two
     return (pushed[None, None], scores[None, None])
 
 

time: 135 us -> 128 us (0.948)
  the two profiles are of different devices: /device:TPU:8 before, /device:TPU:1 now
where the time goes in v11:
time: 128 us; the launch traced here: 126 us
  Pallas kernels  119 us (93%)
  local copies, waits for them, and re-layouts  3.6 us (3%)
  other arithmetic  2.1 us (2%)
  between operations  1.34 us (1%)
    pallas_call x1, Pallas kernels, middle(): pl.pallas_call(functools.partial(middle_kernel, n_row, n_col), out_shape=...  45.9 us
    pallas_call x1, Pallas kernels, gather(): pl.pallas_call(functools.partial(gather_kernel, n), out_shape=jax.ShapeDt...  32.7 us
    pallas_call x1, Pallas kernels, exchange(): pl.pallas_call(functools.partial(exchange_kernel, axis, other_axis, n, sp...  21.7 us
    pallas_call x2, Pallas kernels, tile_products(): pl.pallas_call(functools.partial(products_kernel, flipped, pack), in_spec...  18.7 us

profile of v11, /device:TPU:1, one launch (start us, length us, event | category | flops | bytes accessed | tf_op | source)
XLA Modules:
  0.0 126.0 jit_solution(16617414388768319524)
XLA Ops:
  0.6 0.8 copy.14
  1.4 0.7 reshape_squeeze.11.coords_ref
  2.8 32.7 %shard_map.113.gathered_ref = bf16[32,128,128]{2,1,0:T(8,128)(2,1)} custom-call(bf16[128,128]{1,0:T(8,128)(2,1)} %bitcast.21), custom_call_target="tpu_custom_call" | custom-call | tf_op jit(solution)/shard_map/pallas_call | solution.py:143
  35.5 0.0 copy-start.2
  35.5 8.9 %shard_map.114.parts_ref = bf16[16,128,128]{2,1,0:T(8,128)(2,1)} custom-call(s32[256]{0:T(256)} %reshape_squeeze.11.coords_ref, s32[1]{0:T(128)} %bitcast.17.count_ref, bf16[128,128,128]{2,1,0:T(8,128)(2,1)} %bitcast.19, bf16[32,128,128]{2,1,0:T(8,128)(2,1)} %shard_map.113.gathered_ref), custom_call_target="tpu_custom_call" | custom-call | tf_op jit(solution)/shard_map/pallas_call | solution.py:362
  44.4 0.0 copy-done.2
  44.4 0.7 copy.15.mask_ref
  45.1 45.9 %shard_map.115 = (bf16[128,256]{1,0:T(8,128)(2,1)}, bf16[32,172,128]{2,1,0:T(8,128)(2,1)}) custom-call(bf16[16,128,128]{2,1,0:T(8,128)(2,1)} %shard_map.114.parts_ref, bf16[128,128]{1,0:T(8,128)(2,1)} %bitcast.22, bf16[128,256]{1,0:T(8,128)(2,1)} %weight_one_ref.1, f32[1,256]{1,0:T(1,128)} %bitcast.26, s32[128,1]{1,0:T(8,128)} %copy.15.mask_ref, ...), custom_call_target="tpu_custom_call" | custom-call | tf_op jit(solution)/shard_map/pallas_call | solution.py:230
  91.0 9.8 %shard_map.116.src_ref = bf16[16,172,128]{2,1,0:T(8,128)(2,1)} custom-call(s32[256]{0:T(256)} %reshape_squeeze.11.coords_ref, s32[1]{0:T(128)} %bitcast.18.count_ref, bf16[128,128,128]{2,1,0:T(8,128)(2,1)} %bitcast.20, bf16[32,172,128]{2,1,0:T(8,128)(2,1)} %get-tuple-element.5.gathered_ref), custom_call_target="tpu_custom_call" | custom-call | tf_op jit(solution)/shard_map/pallas_call | solution.py:362
  100.8 0.0 copy-start.1
  100.8 0.0 copy-start
  100.8 21.7 %shard_map.117 = bf16[16,172,128]{2,1,0:T(8,128)(2,1)} custom-call(bf16[16,172,128]{2,1,0:T(8,128)(2,1)} %shard_map.116.src_ref), custom_call_target="tpu_custom_call" | custom-call | tf_op jit(solution)/shard_map/pallas_call | solution.py:261
  122.5 1.2 convert_reduce_fusion
  123.7 0.0 copy-done.1
  123.7 0.9 fusion.1
  124.6 0.7 copy.16
  125.3 0.0 copy-done
  125.3 0.6 copy.19
Async XLA Ops:
  35.5 8.9 %copy-start.2 = (s32[1,1,128]{2,1,0:T(1,128)S(1)}, s32[1,1,128]{2,1,0:T(1,128)}, u32[]{:S(2)}) copy-start(s32[1,1,128]{2,1,0:T(1,128)} %param.14) | copy-start | bytes 1540
  100.8 22.9 %copy-start.1 = (f32[172]{0:T(256)S(1)}, f32[172]{0:T(256)}, u32[]{:S(2)}) copy-start(f32[172]{0:T(256)} %param.19) | copy-start | bytes 2068
  100.8 24.5 %copy-start = (bf16[128,256]{1,0:T(8,128)(2,1)S(1)}, bf16[128,256]{1,0:T(8,128)(2,1)}, u32[]{:S(2)}) copy-start(bf16[128,256]{1,0:T(8,128)(2,1)} %get-tuple-element.4) | copy-start | bytes 196612

commit v12 on v11

--- a/solution.py
+++ b/solution.py
@@ -162,6 +162,7 @@
     weight_two_ref,
     pushed_ref,
     out_ref,
+    own_ref,
     landing_ref,
     col_send,
     col_recv,
@@ -217,7 +218,8 @@
     projected = lax.dot_general(
         weight_two_ref[...], pushed, (((1,), (1,)), ((), ())), preferred_element_type=jnp.float32
     )
-    out_ref[row] = projected.astype(out_ref.dtype)
+    own_ref[...] = projected.astype(own_ref.dtype)
+    out_ref[row] = own_ref[...]
     row_transfer(n_row, out_ref.at[row], out_ref, send_sem, pass_sem, recv_sem)
 
 
@@ -232,9 +234,10 @@
         out_shape=(
             jax.ShapeDtypeStruct(history.shape, history.dtype),
             jax.ShapeDtypeStruct((n_row, classes, nodes), jnp.bfloat16),
+            jax.ShapeDtypeStruct((classes, nodes), jnp.bfloat16),
         ),
         in_specs=[vmem] * 7,
-        out_specs=(vmem, vmem),
+        out_specs=(vmem, vmem, vmem),
         scratch_shapes=[
             pltpu.VMEM(parts.shape, parts.dtype),
             pltpu.SemaphoreType.DMA((n_col,)),
@@ -293,6 +296,31 @@
     tiles = in_blocks(shard, dim, lax.axis_size(axis))
     arrived = lax.all_to_all(tiles, axis, split_axis=0, concat_axis=0, tiled=True)
     return arrived.astype(jnp.float32).sum(axis=0)
+
+
+def final_kernel(n, parts_ref, own_ref, out_ref, landing_ref, send_sem, recv_sem):
+    exchange_kernel("col", "row", n, True, parts_ref, landing_ref, send_sem, recv_sem)
+    total = own_ref[...].astype(jnp.float32)
+    for k in range(n):
+        total = total + landing_ref[k].astype(jnp.float32)
+    out_ref[...] = total
+
+
+def final_sum(parts, own, tag):
+    n = lax.axis_size("col")
+    vmem = pl.BlockSpec(memory_space=pltpu.VMEM)
+    return pl.pallas_call(
+        functools.partial(final_kernel, n),
+        out_shape=jax.ShapeDtypeStruct(own.shape, jnp.float32),
+        in_specs=[vmem, vmem],
+        out_specs=vmem,
+        scratch_shapes=[
+            pltpu.VMEM(parts.shape, parts.dtype),
+            pltpu.SemaphoreType.DMA((n,)),
+            pltpu.SemaphoreType.DMA((n,)),
+        ],
+        compiler_params=pltpu.CompilerParams(collective_id=tag, has_side_effects=True),
+    )(parts, own)
 
 
 def products_kernel(
@@ -389,7 +417,7 @@
     live_total = tile_count[0, 0]
     gathered_input = gather(features[0, 0], 0)
     summed_one = tile_products(gathered_input, tile_set, coord_set, live_total)
-    pushed, gathered_proj = middle(
+    pushed, gathered_proj, own_block = middle(
         summed_one,
         features[0, 0],
         weight_one,
@@ -400,9 +428,7 @@
         1,
     )
     summed_two = tile_products(gathered_proj, tile_set, coord_set, live_total, True)
-    owned_two = exchange(summed_two, "col", True, 3).astype(jnp.float32).sum(axis=0)
-    own_block = gathered_proj[lax.axis_index("row")].astype(jnp.float32)
-    scores = (own_block + owned_two).T + bias_two
+    scores = final_sum(summed_two, own_block, 3).T + bias_two
     return (pushed[None, None], scores[None, None])
 
 

time: 128 us -> 129 us (level)
    pallas_call x2, Pallas kernels: 18.7 us -> 14.9 us  [tile_products(): pl.pallas_call(functools.partial(products_kernel, flipped, pack), in_spec...]
    pallas_call x1, Pallas kernels: 45.9 us -> 49.5 us  [middle(): pl.pallas_call(functools.partial(middle_kernel, n_row, n_col), out_shape=...]
    pallas_call x1, Pallas kernels: 21.7 us -> 23.1 us  [final_sum(): pl.pallas_call(functools.partial(final_kernel, n), out_shape=jax.ShapeDty...]
where the time goes in v12:
time: 129 us; the launch traced here: 127 us
  Pallas kernels  120 us (93%)
  local copies, waits for them, and re-layouts  4.25 us (3%)
  between operations  1.33 us (1%)
    pallas_call x1, Pallas kernels, middle(): pl.pallas_call(functools.partial(middle_kernel, n_row, n_col), out_shape=...  49.5 us
    pallas_call x1, Pallas kernels, gather(): pl.pallas_call(functools.partial(gather_kernel, n), out_shape=jax.ShapeDt...  32.7 us
    pallas_call x1, Pallas kernels, final_sum(): pl.pallas_call(functools.partial(final_kernel, n), out_shape=jax.ShapeDty...  23.1 us
    pallas_call x2, Pallas kernels, tile_products(): pl.pallas_call(functools.partial(products_kernel, flipped, pack), in_spec...  14.9 us

profile of v12, /device:TPU:1, one launch (start us, length us, event | category | flops | bytes accessed | tf_op | source)
XLA Modules:
  0.0 126.8 jit_solution(9639766717518795382)
XLA Ops:
  1.3 0.8 copy.14
  2.1 0.7 reshape_squeeze.11.coords_ref
  2.8 1.4 %copy.15.mask_ref = s32[128,1]{1,0:T(8,128)} copy(s32[128,1]{0,1:T(1,128)} %bitcast.24) | data formatting | bytes 1024 | tf_op jit(solution)/shard_map/reshape;squeeze | solution.py:253
  4.2 32.7 %shard_map.113.gathered_ref = bf16[32,128,128]{2,1,0:T(8,128)(2,1)} custom-call(bf16[128,128]{1,0:T(8,128)(2,1)} %bitcast.18), custom_call_target="tpu_custom_call" | custom-call | tf_op jit(solution)/shard_map/pallas_call | solution.py:143
  36.9 7.1 %shard_map.114.parts_ref = bf16[16,128,128]{2,1,0:T(8,128)(2,1)} custom-call(s32[256]{0:T(256)} %reshape_squeeze.11.coords_ref, s32[1]{0:T(128)} %bitcast.14.count_ref, bf16[128,128,128]{2,1,0:T(8,128)(2,1)} %bitcast.16, bf16[32,128,128]{2,1,0:T(8,128)(2,1)} %shard_map.113.gathered_ref), custom_call_target="tpu_custom_call" | custom-call | tf_op jit(solution)/shard_map/pallas_call | solution.py:390
  43.9 0.0 copy-start.1
  43.9 49.5 %shard_map.115 = (bf16[128,256]{1,0:T(8,128)(2,1)}, bf16[32,172,128]{2,1,0:T(8,128)(2,1)}, bf16[172,128]{1,0:T(8,128)(2,1)}) custom-call(bf16[16,128,128]{2,1,0:T(8,128)(2,1)} %shard_map.114.parts_ref, bf16[128,128]{1,0:T(8,128)(2,1)} %bitcast.19, bf16[128,256]{1,0:T(8,128)(2,1)} %weight_one_ref.1, f32[1,256]{1,0:T(1,128)} %bitcast.23, ...), custom_call_target="tpu_custom_call" | custom-call | tf_op jit(solution)/shard_map/pallas_call | solution.py:232
  93.5 0.0 copy-start
  93.5 7.8 %shard_map.116.parts_ref = bf16[16,172,128]{2,1,0:T(8,128)(2,1)} custom-call(s32[256]{0:T(256)} %reshape_squeeze.11.coords_ref, s32[1]{0:T(128)} %bitcast.15.count_ref, bf16[128,128,128]{2,1,0:T(8,128)(2,1)} %bitcast.17, bf16[32,172,128]{2,1,0:T(8,128)(2,1)} %get-tuple-element.6.gathered_ref), custom_call_target="tpu_custom_call" | custom-call | tf_op jit(solution)/shard_map/pallas_call | solution.py:390
  101.3 23.1 %shard_map.117 = f32[172,128]{1,0:T(8,128)} custom-call(bf16[16,172,128]{2,1,0:T(8,128)(2,1)} %shard_map.116.parts_ref, bf16[172,128]{1,0:T(8,128)(2,1)} %get-tuple-element.7.own_ref), custom_call_target="tpu_custom_call" | custom-call | tf_op jit(solution)/shard_map/pallas_call | solution.py:312
  124.4 0.0 copy-done.1
  124.4 1.0 add_bitcast_fusion
  125.4 0.7 copy.16
  126.1 0.0 copy-done
  126.1 0.6 copy.19
Async XLA Ops:
  43.9 80.5 %copy-start.1 = (f32[172]{0:T(256)S(1)}, f32[172]{0:T(256)}, u32[]{:S(2)}) copy-start(f32[172]{0:T(256)} %param.19) | copy-start | bytes 2068
  93.5 32.7 %copy-start = (bf16[128,256]{1,0:T(8,128)(2,1)S(1)}, bf16[128,256]{1,0:T(8,128)(2,1)}, u32[]{:S(2)}) copy-start(bf16[128,256]{1,0:T(8,128)(2,1)} %get-tuple-element.5) | copy-start | bytes 196612

commit v13 on v11

--- a/solution.py
+++ b/solution.py
@@ -296,8 +296,29 @@
 
 
 def products_kernel(
-    flipped, pack, coords_ref, count_ref, tiles_ref, gathered_ref, out_ref, order_ref, bounds_ref, cursor_ref
+    flipped,
+    pack,
+    coords_ref,
+    count_ref,
+    tiles_hbm,
+    gathered_ref,
+    out_ref,
+    order_ref,
+    bounds_ref,
+    cursor_ref,
+    tiles_ref,
+    load_sem,
 ):
+    chunks = load_sem.shape[0]
+    size = tiles_ref.shape[0] // chunks
+    loads = [
+        pltpu.make_async_copy(
+            tiles_hbm.at[pl.ds(c * size, size)], tiles_ref.at[pl.ds(c * size, size)], load_sem.at[c]
+        )
+        for c in range(chunks)
+    ]
+    for load in loads:
+        load.start()
     blocks = out_ref.shape[0]
     live = count_ref[0]
     for target in range(blocks + 1):
@@ -321,6 +342,8 @@
         return carry
 
     lax.fori_loop(0, live, place, 0)
+    for load in loads:
+        load.wait()
 
     def product(first, end, total):
         tiles, sources = [], []
@@ -361,13 +384,15 @@
     smem = pl.BlockSpec(memory_space=pltpu.SMEM)
     return pl.pallas_call(
         functools.partial(products_kernel, flipped, pack),
-        in_specs=[smem, smem, vmem, vmem],
+        in_specs=[smem, smem, pl.BlockSpec(memory_space=pl.ANY), vmem],
         out_specs=vmem,
         out_shape=jax.ShapeDtypeStruct((row_blocks, *block_shape), jnp.bfloat16),
         scratch_shapes=[
             pltpu.SMEM((slots,), jnp.int32),
             pltpu.SMEM((row_blocks + 1,), jnp.int32),
             pltpu.SMEM((row_blocks,), jnp.int32),
+            pltpu.VMEM(tiles.shape, tiles.dtype),
+            pltpu.SemaphoreType.DMA((8,)),
         ],
     )(coords.reshape(-1), live_total.reshape(1), tiles, gathered)
 

time: 128 us -> 128 us (level)
  no operation moved by 1% of the time
where the time goes in v13:
time: 128 us; the launch traced here: 127 us
  Pallas kernels  119 us (93%)
  local copies, waits for them, and re-layouts  3.61 us (3%)
  other arithmetic  2.1 us (2%)
  between operations  1.37 us (1%)
    pallas_call x1, Pallas kernels, middle(): pl.pallas_call(functools.partial(middle_kernel, n_row, n_col), out_shape=...  45.6 us
    pallas_call x1, Pallas kernels, gather(): pl.pallas_call(functools.partial(gather_kernel, n), out_shape=jax.ShapeDt...  32.7 us
    pallas_call x1, Pallas kernels, exchange(): pl.pallas_call(functools.partial(exchange_kernel, axis, other_axis, n, sp...  22.3 us
    pallas_call x2, Pallas kernels, tile_products(): pl.pallas_call(functools.partial(products_kernel, flipped, pack), in_spec...  18.8 us

profile of v13, /device:TPU:1, one launch (start us, length us, event | category | flops | bytes accessed | tf_op | source)
XLA Modules:
  0.0 126.5 jit_solution(675876495169561082)
XLA Ops:
  0.6 0.8 copy.14
  1.4 0.7 reshape_squeeze.11.coords_ref
  2.8 32.7 %shard_map.113.gathered_ref = bf16[32,128,128]{2,1,0:T(8,128)(2,1)} custom-call(bf16[128,128]{1,0:T(8,128)(2,1)} %bitcast.21), custom_call_target="tpu_custom_call" | custom-call | tf_op jit(solution)/shard_map/pallas_call | solution.py:143
  35.5 0.0 copy-start.2
  35.5 8.9 %shard_map.114.parts_ref = bf16[16,128,128]{2,1,0:T(8,128)(2,1)} custom-call(s32[256]{0:T(256)} %reshape_squeeze.11.coords_ref, s32[1]{0:T(128)} %bitcast.17.count_ref, bf16[128,128,128]{2,1,0:T(8,128)(2,1)} %bitcast.19, bf16[32,128,128]{2,1,0:T(8,128)(2,1)} %shard_map.113.gathered_ref), custom_call_target="tpu_custom_call" | custom-call | tf_op jit(solution)/shard_map/pallas_call | solution.py:385
  44.4 0.0 copy-done.2
  44.4 0.7 copy.15.mask_ref
  45.2 45.6 %shard_map.115 = (bf16[128,256]{1,0:T(8,128)(2,1)}, bf16[32,172,128]{2,1,0:T(8,128)(2,1)}) custom-call(bf16[16,128,128]{2,1,0:T(8,128)(2,1)} %shard_map.114.parts_ref, bf16[128,128]{1,0:T(8,128)(2,1)} %bitcast.22, bf16[128,256]{1,0:T(8,128)(2,1)} %weight_one_ref.1, f32[1,256]{1,0:T(1,128)} %bitcast.26, s32[128,1]{1,0:T(8,128)} %copy.15.mask_ref, ...), custom_call_target="tpu_custom_call" | custom-call | tf_op jit(solution)/shard_map/pallas_call | solution.py:230
  90.8 9.9 %shard_map.116.src_ref = bf16[16,172,128]{2,1,0:T(8,128)(2,1)} custom-call(s32[256]{0:T(256)} %reshape_squeeze.11.coords_ref, s32[1]{0:T(128)} %bitcast.18.count_ref, bf16[128,128,128]{2,1,0:T(8,128)(2,1)} %bitcast.20, bf16[32,172,128]{2,1,0:T(8,128)(2,1)} %get-tuple-element.5.gathered_ref), custom_call_target="tpu_custom_call" | custom-call | tf_op jit(solution)/shard_map/pallas_call | solution.py:385
  100.7 0.0 copy-start.1
  100.7 0.0 copy-start
  100.7 22.3 %shard_map.117 = bf16[16,172,128]{2,1,0:T(8,128)(2,1)} custom-call(bf16[16,172,128]{2,1,0:T(8,128)(2,1)} %shard_map.116.src_ref), custom_call_target="tpu_custom_call" | custom-call | tf_op jit(solution)/shard_map/pallas_call | solution.py:261
  123.0 1.2 convert_reduce_fusion
  124.2 0.0 copy-done.1
  124.3 0.9 fusion.1
  125.1 0.7 copy.16
  125.9 0.0 copy-done
  125.9 0.6 copy.19
Async XLA Ops:
  35.5 8.9 %copy-start.2 = (s32[1,1,128]{2,1,0:T(1,128)S(1)}, s32[1,1,128]{2,1,0:T(1,128)}, u32[]{:S(2)}) copy-start(s32[1,1,128]{2,1,0:T(1,128)} %param.14) | copy-start | bytes 1540
  100.7 23.6 %copy-start.1 = (f32[172]{0:T(256)S(1)}, f32[172]{0:T(256)}, u32[]{:S(2)}) copy-start(f32[172]{0:T(256)} %param.19) | copy-start | bytes 2068
  100.7 25.2 %copy-start = (bf16[128,256]{1,0:T(8,128)(2,1)S(1)}, bf16[128,256]{1,0:T(8,128)(2,1)}, u32[]{:S(2)}) copy-start(bf16[128,256]{1,0:T(8,128)(2,1)} %get-tuple-element.4) | copy-start | bytes 196612

commit v14 on v13

--- a/solution.py
+++ b/solution.py
@@ -70,16 +70,26 @@
     return me, lax.axis_index("col"), me + 1 - 2 * lax.rem(me, 2)
 
 
+def near_first(n):
+    rings = n // 4
+    order = sorted(range(1, rings), key=lambda d: (min(d, rings - d), d))
+    return [(d, 0) for d in order] + [(d, 1) for d in [0] + order]
+
+
+def row_peer(me, n, shift):
+    rings = n // 4
+    ring, half_index = me // 4, lax.rem(me // 2, 2)
+    ring = lax.rem(ring + shift[0], rings)
+    half_index = lax.rem(half_index + shift[1], 2)
+    return (ring * 2 + half_index) * 2 + lax.rem(me, 2)
+
+
 def row_greet(barrier, n):
     me, other, twin = row_partners()
     pl.semaphore_signal(barrier, 1, device_id=(twin, other), device_id_type=MESH_ID)
-
-    def greet(step, carry):
-        peer = lax.rem(me + 2 * step, n)
+    for shift in near_first(n):
+        peer = row_peer(me, n, shift)
         pl.semaphore_signal(barrier, 1, device_id=(peer, other), device_id_type=MESH_ID)
-        return carry
-
-    lax.fori_loop(1, n // 2, greet, 0)
     return n // 2
 
 
@@ -97,35 +107,20 @@
             device_id_type=MESH_ID,
         )
 
-    def peer(step):
-        return lax.rem(me + 2 * step, n)
-
-    def far(step):
-        return lax.rem(twin + 2 * step, n)
-
-    def send(step, carry):
-        copy(src_ref, me, send_sem, peer(step)).start()
-        return carry
-
-    lax.fori_loop(1, half, send, 0)
+    shifts = near_first(n)
+    for shift in shifts:
+        copy(src_ref, me, send_sem, row_peer(me, n, shift)).start()
     copy(src_ref, me, send_sem, twin).start()
-
-    def relay(step, carry):
-        k = peer(step)
+    for shift in shifts:
+        k = row_peer(me, n, shift)
         copy(src_ref, k, send_sem, k).wait_recv()
         copy(out_ref.at[k], k, pass_sem, twin).start()
-        return carry
-
-    lax.fori_loop(1, half, relay, 0)
-
-    def finish(step, carry):
-        k = peer(step)
+    for shift in shifts:
+        k = row_peer(me, n, shift)
         copy(src_ref, me, send_sem, k).wait_send()
         copy(out_ref.at[k], k, pass_sem, twin).wait_send()
-        copy(src_ref, far(step), send_sem, twin).wait_recv()
-        return carry
-
-    lax.fori_loop(1, half, finish, 0)
+        far = row_peer(twin, n, shift)
+        copy(src_ref, far, send_sem, twin).wait_recv()
     copy(src_ref, me, send_sem, twin).wait_send()
     copy(src_ref, twin, send_sem, twin).wait_recv()
 

time: 128 us -> 131 us (1.023)
  Pallas kernels: 119 us -> 123 us
    pallas_call x1, Pallas kernels: 45.6 us -> 47.9 us  [middle(): pl.pallas_call(functools.partial(middle_kernel, n_row, n_col), out_shape=...]
    pallas_call x2, Pallas kernels: 18.8 us -> 17.2 us  [tile_products(): pl.pallas_call(functools.partial(products_kernel, flipped, pack), in_spec...]
    pallas_call x1, Pallas kernels: 32.7 us -> 34.1 us  [gather(): pl.pallas_call(functools.partial(gather_kernel, n), out_shape=jax.ShapeDt...]
    pallas_call x1, Pallas kernels: 22.3 us -> 23.7 us  [exchange(): pl.pallas_call(functools.partial(exchange_kernel, axis, other_axis, n, sp...]
where the time goes in v14:
time: 131 us; the launch traced here: 130 us
  Pallas kernels  123 us (94%)
  local copies, waits for them, and re-layouts  3.61 us (3%)
  other arithmetic  2.1 us (2%)
  between operations  1.37 us (1%)
    pallas_call x1, Pallas kernels, middle(): pl.pallas_call(functools.partial(middle_kernel, n_row, n_col), out_shape=...  47.9 us
    pallas_call x1, Pallas kernels, gather(): pl.pallas_call(functools.partial(gather_kernel, n), out_shape=jax.ShapeDt...  34.1 us
    pallas_call x1, Pallas kernels, exchange(): pl.pallas_call(functools.partial(exchange_kernel, axis, other_axis, n, sp...  23.7 us
    pallas_call x2, Pallas kernels, tile_products(): pl.pallas_call(functools.partial(products_kernel, flipped, pack), in_spec...  17.2 us

profile of v14, /device:TPU:1, one launch (start us, length us, event | category | flops | bytes accessed | tf_op | source)
XLA Modules:
  0.0 130.0 jit_solution(16229745678460225609)
XLA Ops:
  0.6 0.8 copy.14
  1.4 0.7 reshape_squeeze.11.coords_ref
  2.8 34.1 %shard_map.113.gathered_ref = bf16[32,128,128]{2,1,0:T(8,128)(2,1)} custom-call(bf16[128,128]{1,0:T(8,128)(2,1)} %bitcast.21), custom_call_target="tpu_custom_call" | custom-call | tf_op jit(solution)/shard_map/pallas_call | solution.py:138
  36.9 0.0 copy-start.2
  36.9 8.2 %shard_map.114.parts_ref = bf16[16,128,128]{2,1,0:T(8,128)(2,1)} custom-call(s32[256]{0:T(256)} %reshape_squeeze.11.coords_ref, s32[1]{0:T(128)} %bitcast.17.count_ref, bf16[128,128,128]{2,1,0:T(8,128)(2,1)} %bitcast.19, bf16[32,128,128]{2,1,0:T(8,128)(2,1)} %shard_map.113.gathered_ref), custom_call_target="tpu_custom_call" | custom-call | tf_op jit(solution)/shard_map/pallas_call | solution.py:380
  45.1 0.0 copy-done.2
  45.1 0.7 copy.15.mask_ref
  45.8 47.9 %shard_map.115 = (bf16[128,256]{1,0:T(8,128)(2,1)}, bf16[32,172,128]{2,1,0:T(8,128)(2,1)}) custom-call(bf16[16,128,128]{2,1,0:T(8,128)(2,1)} %shard_map.114.parts_ref, bf16[128,128]{1,0:T(8,128)(2,1)} %bitcast.22, bf16[128,256]{1,0:T(8,128)(2,1)} %weight_one_ref.1, f32[1,256]{1,0:T(1,128)} %bitcast.26, s32[128,1]{1,0:T(8,128)} %copy.15.mask_ref, ...), custom_call_target="tpu_custom_call" | custom-call | tf_op jit(solution)/shard_map/pallas_call | solution.py:225
  93.8 9.0 %shard_map.116.src_ref = bf16[16,172,128]{2,1,0:T(8,128)(2,1)} custom-call(s32[256]{0:T(256)} %reshape_squeeze.11.coords_ref, s32[1]{0:T(128)} %bitcast.18.count_ref, bf16[128,128,128]{2,1,0:T(8,128)(2,1)} %bitcast.20, bf16[32,172,128]{2,1,0:T(8,128)(2,1)} %get-tuple-element.5.gathered_ref), custom_call_target="tpu_custom_call" | custom-call | tf_op jit(solution)/shard_map/pallas_call | solution.py:380
  102.8 0.0 copy-start.1
  102.8 0.0 copy-start
  102.8 23.7 %shard_map.117 = bf16[16,172,128]{2,1,0:T(8,128)(2,1)} custom-call(bf16[16,172,128]{2,1,0:T(8,128)(2,1)} %shard_map.116.src_ref), custom_call_target="tpu_custom_call" | custom-call | tf_op jit(solution)/shard_map/pallas_call | solution.py:256
  126.6 1.2 convert_reduce_fusion
  127.8 0.0 copy-done.1
  127.8 0.9 fusion.1
  128.7 0.7 copy.16
  129.4 0.0 copy-done
  129.4 0.6 copy.19
Async XLA Ops:
  36.9 8.2 %copy-start.2 = (s32[1,1,128]{2,1,0:T(1,128)S(1)}, s32[1,1,128]{2,1,0:T(1,128)}, u32[]{:S(2)}) copy-start(s32[1,1,128]{2,1,0:T(1,128)} %param.14) | copy-start | bytes 1540
  102.8 25.0 %copy-start.1 = (f32[172]{0:T(256)S(1)}, f32[172]{0:T(256)}, u32[]{:S(2)}) copy-start(f32[172]{0:T(256)} %param.19) | copy-start | bytes 2068
  102.8 26.6 %copy-start = (bf16[128,256]{1,0:T(8,128)(2,1)S(1)}, bf16[128,256]{1,0:T(8,128)(2,1)}, u32[]{:S(2)}) copy-start(bf16[128,256]{1,0:T(8,128)(2,1)} %get-tuple-element.4) | copy-start | bytes 196612

commit v15 on v14

--- a/solution.py
+++ b/solution.py
@@ -108,7 +108,7 @@
         )
 
     shifts = near_first(n)
-    for shift in shifts:
+    for shift in reversed(shifts):
         copy(src_ref, me, send_sem, row_peer(me, n, shift)).start()
     copy(src_ref, me, send_sem, twin).start()
     for shift in shifts:

time: 131 us -> 133 us (1.015)
  Pallas kernels: 123 us -> 126 us
    pallas_call x1, Pallas kernels: 23.7 us -> 26.8 us  [exchange(): pl.pallas_call(functools.partial(exchange_kernel, axis, other_axis, n, sp...]
    pallas_call x1, Pallas kernels: 47.9 us -> 49.8 us  [middle(): pl.pallas_call(functools.partial(middle_kernel, n_row, n_col), out_shape=...]
    pallas_call x1, Pallas kernels: 34.1 us -> 32.7 us  [gather(): pl.pallas_call(functools.partial(gather_kernel, n), out_shape=jax.ShapeDt...]
where the time goes in v15:
time: 133 us
  Pallas kernels  126 us (95%)
  local copies, waits for them, and re-layouts  3.61 us (3%)
  other arithmetic  2.1 us (2%)
  between operations  1.37 us (1%)
    pallas_call x1, Pallas kernels, middle(): pl.pallas_call(functools.partial(middle_kernel, n_row, n_col), out_shape=...  49.8 us
    pallas_call x1, Pallas kernels, gather(): pl.pallas_call(functools.partial(gather_kernel, n), out_shape=jax.ShapeDt...  32.7 us
    pallas_call x1, Pallas kernels, exchange(): pl.pallas_call(functools.partial(exchange_kernel, axis, other_axis, n, sp...  26.8 us
    pallas_call x2, Pallas kernels, tile_products(): pl.pallas_call(functools.partial(products_kernel, flipped, pack), in_spec...  16.2 us

profile of v15, /device:TPU:1, one launch (start us, length us, event | category | flops | bytes accessed | tf_op | source)
XLA Modules:
  0.0 132.6 jit_solution(5582345999478661162)
XLA Ops:
  0.6 0.8 copy.14
  1.4 0.7 reshape_squeeze.11.coords_ref
  2.8 32.7 %shard_map.113.gathered_ref = bf16[32,128,128]{2,1,0:T(8,128)(2,1)} custom-call(bf16[128,128]{1,0:T(8,128)(2,1)} %bitcast.21), custom_call_target="tpu_custom_call" | custom-call | tf_op jit(solution)/shard_map/pallas_call | solution.py:138
  35.5 0.0 copy-start.2
  35.5 7.7 %shard_map.114.parts_ref = bf16[16,128,128]{2,1,0:T(8,128)(2,1)} custom-call(s32[256]{0:T(256)} %reshape_squeeze.11.coords_ref, s32[1]{0:T(128)} %bitcast.17.count_ref, bf16[128,128,128]{2,1,0:T(8,128)(2,1)} %bitcast.19, bf16[32,128,128]{2,1,0:T(8,128)(2,1)} %shard_map.113.gathered_ref), custom_call_target="tpu_custom_call" | custom-call | tf_op jit(solution)/shard_map/pallas_call | solution.py:380
  43.2 0.0 copy-done.2
  43.3 0.7 copy.15.mask_ref
  44.0 49.8 %shard_map.115 = (bf16[128,256]{1,0:T(8,128)(2,1)}, bf16[32,172,128]{2,1,0:T(8,128)(2,1)}) custom-call(bf16[16,128,128]{2,1,0:T(8,128)(2,1)} %shard_map.114.parts_ref, bf16[128,128]{1,0:T(8,128)(2,1)} %bitcast.22, bf16[128,256]{1,0:T(8,128)(2,1)} %weight_one_ref.1, f32[1,256]{1,0:T(1,128)} %bitcast.26, s32[128,1]{1,0:T(8,128)} %copy.15.mask_ref, ...), custom_call_target="tpu_custom_call" | custom-call | tf_op jit(solution)/shard_map/pallas_call | solution.py:225
  93.8 8.5 %shard_map.116.src_ref = bf16[16,172,128]{2,1,0:T(8,128)(2,1)} custom-call(s32[256]{0:T(256)} %reshape_squeeze.11.coords_ref, s32[1]{0:T(128)} %bitcast.18.count_ref, bf16[128,128,128]{2,1,0:T(8,128)(2,1)} %bitcast.20, bf16[32,172,128]{2,1,0:T(8,128)(2,1)} %get-tuple-element.5.gathered_ref), custom_call_target="tpu_custom_call" | custom-call | tf_op jit(solution)/shard_map/pallas_call | solution.py:380
  102.4 0.0 copy-start.1
  102.4 0.0 copy-start
  102.4 26.8 %shard_map.117 = bf16[16,172,128]{2,1,0:T(8,128)(2,1)} custom-call(bf16[16,172,128]{2,1,0:T(8,128)(2,1)} %shard_map.116.src_ref), custom_call_target="tpu_custom_call" | custom-call | tf_op jit(solution)/shard_map/pallas_call | solution.py:256
  129.1 1.2 convert_reduce_fusion
  130.4 0.0 copy-done.1
  130.4 0.9 fusion.1
  131.3 0.7 copy.16
  132.0 0.0 copy-done
  132.0 0.6 copy.19
Async XLA Ops:
  35.5 7.7 %copy-start.2 = (s32[1,1,128]{2,1,0:T(1,128)S(1)}, s32[1,1,128]{2,1,0:T(1,128)}, u32[]{:S(2)}) copy-start(s32[1,1,128]{2,1,0:T(1,128)} %param.14) | copy-start | bytes 1540
  102.4 28.0 %copy-start.1 = (f32[172]{0:T(256)S(1)}, f32[172]{0:T(256)}, u32[]{:S(2)}) copy-start(f32[172]{0:T(256)} %param.19) | copy-start | bytes 2068
  102.4 29.6 %copy-start = (bf16[128,256]{1,0:T(8,128)(2,1)S(1)}, bf16[128,256]{1,0:T(8,128)(2,1)}, u32[]{:S(2)}) copy-start(bf16[128,256]{1,0:T(8,128)(2,1)} %get-tuple-element.4) | copy-start | bytes 196612

commit v16 on v13

--- a/solution.py
+++ b/solution.py
@@ -320,12 +320,13 @@
     for load in loads:
         load.start()
     blocks = out_ref.shape[0]
+    sources_count = gathered_ref.shape[0]
     live = count_ref[0]
     for target in range(blocks + 1):
         bounds_ref[target] = 0
 
     def count(slot, carry):
-        target = coords_ref[2 * slot]
+        target = coords_ref[slot] // sources_count
         bounds_ref[target + 1] = bounds_ref[target + 1] + 1
         return carry
 
@@ -335,7 +336,7 @@
         cursor_ref[target] = bounds_ref[target]
 
     def place(slot, carry):
-        target = coords_ref[2 * slot]
+        target = coords_ref[slot] // sources_count
         position = cursor_ref[target]
         order_ref[position] = slot
         cursor_ref[target] = position + 1
@@ -351,7 +352,7 @@
             slot = order_ref[jnp.minimum(first + offset, end - 1)]
             tile = tiles_ref[slot]
             tiles.append(jnp.where(first + offset < end, tile, jnp.zeros_like(tile)))
-            sources.append(gathered_ref[coords_ref[2 * slot + 1]])
+            sources.append(gathered_ref[coords_ref[slot] % sources_count])
         if flipped:
             return total + lax.dot_general(
                 jnp.concatenate(sources, axis=1),
@@ -394,7 +395,7 @@
             pltpu.VMEM(tiles.shape, tiles.dtype),
             pltpu.SemaphoreType.DMA((8,)),
         ],
-    )(coords.reshape(-1), live_total.reshape(1), tiles, gathered)
+    )(coords, live_total.reshape(1), tiles, gathered)
 
 
 def on_device(
@@ -410,7 +411,7 @@
     bias_two,
 ):
     tile_set = tiles[0, 0]
-    coord_set = tile_coords[0, 0]
+    coord_set = tile_coords[0, 0, :, 0] * lax.axis_size("row") + tile_coords[0, 0, :, 1]
     live_total = tile_count[0, 0]
     gathered_input = gather(features[0, 0], 0)
     summed_one = tile_products(gathered_input, tile_set, coord_set, live_total)

time: 128 us -> 129 us (level)
  Pallas kernels: 119 us -> 121 us
  local copies, waits for them, and re-layouts: 3.61 us -> 2.12 us
    pallas_call x2, Pallas kernels: 18.8 us -> 11.2 us  [tile_products(): pl.pallas_call(functools.partial(products_kernel, flipped, pack), in_spec...]
    pallas_call x1, Pallas kernels: 45.6 us -> 50.7 us  [middle(): pl.pallas_call(functools.partial(middle_kernel, n_row, n_col), out_shape=...]
    pallas_call x1, Pallas kernels: 22.3 us -> 26.7 us  [exchange(): pl.pallas_call(functools.partial(exchange_kernel, axis, other_axis, n, sp...]
where the time goes in v16:
time: 129 us; the launch traced here: 128 us
  Pallas kernels  121 us (94%)
  other arithmetic  3.37 us (3%)
  local copies, waits for them, and re-layouts  2.12 us (2%)
  between operations  1.37 us (1%)
    pallas_call x1, Pallas kernels, middle(): pl.pallas_call(functools.partial(middle_kernel, n_row, n_col), out_shape=...  50.7 us
    pallas_call x1, Pallas kernels, gather(): pl.pallas_call(functools.partial(gather_kernel, n), out_shape=jax.ShapeDt...  32.7 us
    pallas_call x1, Pallas kernels, exchange(): pl.pallas_call(functools.partial(exchange_kernel, axis, other_axis, n, sp...  26.7 us
    pallas_call x2, Pallas kernels, tile_products(): pl.pallas_call(functools.partial(products_kernel, flipped, pack), in_spec...  11.2 us

profile of v16, /device:TPU:1, one launch (start us, length us, event | category | flops | bytes accessed | tf_op | source)
XLA Modules:
  0.0 128.1 jit_solution(401662017396812589)
XLA Ops:
  0.6 1.3 add_bitcast_fusion.coords_ref
  2.5 32.7 %shard_map.113.gathered_ref = bf16[32,128,128]{2,1,0:T(8,128)(2,1)} custom-call(bf16[128,128]{1,0:T(8,128)(2,1)} %bitcast.21), custom_call_target="tpu_custom_call" | custom-call | tf_op jit(solution)/shard_map/pallas_call | solution.py:143
  35.3 0.0 copy-start.2
  35.3 5.4 %shard_map.114.parts_ref = bf16[16,128,128]{2,1,0:T(8,128)(2,1)} custom-call(s32[128]{0:T(128)} %add_bitcast_fusion.coords_ref, s32[1]{0:T(128)} %bitcast.17.count_ref, bf16[128,128,128]{2,1,0:T(8,128)(2,1)} %bitcast.19, bf16[32,128,128]{2,1,0:T(8,128)(2,1)} %shard_map.113.gathered_ref), custom_call_target="tpu_custom_call" | custom-call | tf_op jit(solution)/shard_map/pallas_call | solution.py:386
  40.7 0.0 copy-done.2
  40.7 0.7 copy.12.mask_ref
  41.5 50.7 %shard_map.115 = (bf16[128,256]{1,0:T(8,128)(2,1)}, bf16[32,172,128]{2,1,0:T(8,128)(2,1)}) custom-call(bf16[16,128,128]{2,1,0:T(8,128)(2,1)} %shard_map.114.parts_ref, bf16[128,128]{1,0:T(8,128)(2,1)} %bitcast.22, bf16[128,256]{1,0:T(8,128)(2,1)} %weight_one_ref.1, f32[1,256]{1,0:T(1,128)} %bitcast.26, s32[128,1]{1,0:T(8,128)} %copy.12.mask_ref, ...), custom_call_target="tpu_custom_call" | custom-call | tf_op jit(solution)/shard_map/pallas_call | solution.py:230
  92.2 5.8 %shard_map.116.src_ref = bf16[16,172,128]{2,1,0:T(8,128)(2,1)} custom-call(s32[128]{0:T(128)} %add_bitcast_fusion.coords_ref, s32[1]{0:T(128)} %bitcast.18.count_ref, bf16[128,128,128]{2,1,0:T(8,128)(2,1)} %bitcast.20, bf16[32,172,128]{2,1,0:T(8,128)(2,1)} %get-tuple-element.5.gathered_ref), custom_call_target="tpu_custom_call" | custom-call | tf_op jit(solution)/shard_map/pallas_call | solution.py:386
  98.0 0.0 copy-start.1
  98.0 0.0 copy-start
  98.0 26.7 %shard_map.117 = bf16[16,172,128]{2,1,0:T(8,128)(2,1)} custom-call(bf16[16,172,128]{2,1,0:T(8,128)(2,1)} %shard_map.116.src_ref), custom_call_target="tpu_custom_call" | custom-call | tf_op jit(solution)/shard_map/pallas_call | solution.py:261
  124.6 1.2 convert_reduce_fusion
  125.9 0.0 copy-done.1
  125.9 0.9 fusion.1
  126.8 0.7 copy.13
  127.5 0.0 copy-done
  127.5 0.6 copy.16
Async XLA Ops:
  35.3 5.5 %copy-start.2 = (s32[1,1,128]{2,1,0:T(1,128)S(1)}, s32[1,1,128]{2,1,0:T(1,128)}, u32[]{:S(2)}) copy-start(s32[1,1,128]{2,1,0:T(1,128)} %param.14) | copy-start | bytes 1540
  98.0 27.9 %copy-start.1 = (f32[172]{0:T(256)S(1)}, f32[172]{0:T(256)}, u32[]{:S(2)}) copy-start(f32[172]{0:T(256)} %param.19) | copy-start | bytes 2068
  98.0 29.5 %copy-start = (bf16[128,256]{1,0:T(8,128)(2,1)S(1)}, bf16[128,256]{1,0:T(8,128)(2,1)}, u32[]{:S(2)}) copy-start(bf16[128,256]{1,0:T(8,128)(2,1)} %get-tuple-element.4) | copy-start | bytes 196612

commit v17 on v13

--- a/solution.py
+++ b/solution.py
@@ -310,13 +310,15 @@
     load_sem,
 ):
     chunks = load_sem.shape[0]
-    size = tiles_ref.shape[0] // chunks
+    size = (tiles_ref.shape[0] - 1) // chunks
     loads = [
         pltpu.make_async_copy(
             tiles_hbm.at[pl.ds(c * size, size)], tiles_ref.at[pl.ds(c * size, size)], load_sem.at[c]
         )
         for c in range(chunks)
     ]
+    blank = chunks * size
+    tiles_ref[blank] = jnp.zeros(tiles_ref.shape[1:], tiles_ref.dtype)
     for load in loads:
         load.start()
     blocks = out_ref.shape[0]
@@ -349,8 +351,7 @@
         tiles, sources = [], []
         for offset in range(pack):
             slot = order_ref[jnp.minimum(first + offset, end - 1)]
-            tile = tiles_ref[slot]
-            tiles.append(jnp.where(first + offset < end, tile, jnp.zeros_like(tile)))
+            tiles.append(tiles_ref[jnp.where(first + offset < end, slot, blank)])
             sources.append(gathered_ref[coords_ref[2 * slot + 1]])
         if flipped:
             return total + lax.dot_general(
@@ -391,7 +392,7 @@
             pltpu.SMEM((slots,), jnp.int32),
             pltpu.SMEM((row_blocks + 1,), jnp.int32),
             pltpu.SMEM((row_blocks,), jnp.int32),
-            pltpu.VMEM(tiles.shape, tiles.dtype),
+            pltpu.VMEM((slots + 1, *tiles.shape[1:]), tiles.dtype),
             pltpu.SemaphoreType.DMA((8,)),
         ],
     )(coords.reshape(-1), live_total.reshape(1), tiles, gathered)

time: 128 us -> 129 us (level)
  Pallas kernels: 119 us -> 121 us
    pallas_call x1, Pallas kernels: 22.3 us -> 23.8 us  [exchange(): pl.pallas_call(functools.partial(exchange_kernel, axis, other_axis, n, sp...]
where the time goes in v17:
time: 129 us; the launch traced here: 128 us
  Pallas kernels  121 us (94%)
  local copies, waits for them, and re-layouts  3.61 us (3%)
  other arithmetic  2.1 us (2%)
  between operations  1.37 us (1%)
    pallas_call x1, Pallas kernels, middle(): pl.pallas_call(functools.partial(middle_kernel, n_row, n_col), out_shape=...  45.8 us
    pallas_call x1, Pallas kernels, gather(): pl.pallas_call(functools.partial(gather_kernel, n), out_shape=jax.ShapeDt...  32.7 us
    pallas_call x1, Pallas kernels, exchange(): pl.pallas_call(functools.partial(exchange_kernel, axis, other_axis, n, sp...  23.8 us
    pallas_call x2, Pallas kernels, tile_products(): pl.pallas_call(functools.partial(products_kernel, flipped, pack), in_spec...  18.7 us

profile of v17, /device:TPU:1, one launch (start us, length us, event | category | flops | bytes accessed | tf_op | source)
XLA Modules:
  0.0 128.1 jit_solution(12007092018506809501)
XLA Ops:
  0.6 0.8 copy.14
  1.4 0.7 reshape_squeeze.11.coords_ref
  2.8 32.7 %shard_map.113.gathered_ref = bf16[32,128,128]{2,1,0:T(8,128)(2,1)} custom-call(bf16[128,128]{1,0:T(8,128)(2,1)} %bitcast.21), custom_call_target="tpu_custom_call" | custom-call | tf_op jit(solution)/shard_map/pallas_call | solution.py:143
  35.5 0.0 copy-start.2
  35.5 8.8 %shard_map.114.parts_ref = bf16[16,128,128]{2,1,0:T(8,128)(2,1)} custom-call(s32[256]{0:T(256)} %reshape_squeeze.11.coords_ref, s32[1]{0:T(128)} %bitcast.17.count_ref, bf16[128,128,128]{2,1,0:T(8,128)(2,1)} %bitcast.19, bf16[32,128,128]{2,1,0:T(8,128)(2,1)} %shard_map.113.gathered_ref), custom_call_target="tpu_custom_call" | custom-call | tf_op jit(solution)/shard_map/pallas_call | solution.py:386
  44.3 0.0 copy-done.2
  44.3 0.7 copy.15.mask_ref
  45.1 45.8 %shard_map.115 = (bf16[128,256]{1,0:T(8,128)(2,1)}, bf16[32,172,128]{2,1,0:T(8,128)(2,1)}) custom-call(bf16[16,128,128]{2,1,0:T(8,128)(2,1)} %shard_map.114.parts_ref, bf16[128,128]{1,0:T(8,128)(2,1)} %bitcast.22, bf16[128,256]{1,0:T(8,128)(2,1)} %weight_one_ref.1, f32[1,256]{1,0:T(1,128)} %bitcast.26, s32[128,1]{1,0:T(8,128)} %copy.15.mask_ref, ...), custom_call_target="tpu_custom_call" | custom-call | tf_op jit(solution)/shard_map/pallas_call | solution.py:230
  90.9 9.8 %shard_map.116.src_ref = bf16[16,172,128]{2,1,0:T(8,128)(2,1)} custom-call(s32[256]{0:T(256)} %reshape_squeeze.11.coords_ref, s32[1]{0:T(128)} %bitcast.18.count_ref, bf16[128,128,128]{2,1,0:T(8,128)(2,1)} %bitcast.20, bf16[32,172,128]{2,1,0:T(8,128)(2,1)} %get-tuple-element.5.gathered_ref), custom_call_target="tpu_custom_call" | custom-call | tf_op jit(solution)/shard_map/pallas_call | solution.py:386
  100.8 0.0 copy-start.1
  100.8 0.0 copy-start
  100.8 23.8 %shard_map.117 = bf16[16,172,128]{2,1,0:T(8,128)(2,1)} custom-call(bf16[16,172,128]{2,1,0:T(8,128)(2,1)} %shard_map.116.src_ref), custom_call_target="tpu_custom_call" | custom-call | tf_op jit(solution)/shard_map/pallas_call | solution.py:261
  124.6 1.2 convert_reduce_fusion
  125.8 0.0 copy-done.1
  125.9 0.9 fusion.1
  126.7 0.7 copy.16
  127.5 0.0 copy-done
  127.5 0.6 copy.19
Async XLA Ops:
  35.5 8.9 %copy-start.2 = (s32[1,1,128]{2,1,0:T(1,128)S(1)}, s32[1,1,128]{2,1,0:T(1,128)}, u32[]{:S(2)}) copy-start(s32[1,1,128]{2,1,0:T(1,128)} %param.14) | copy-start | bytes 1540
  100.8 25.1 %copy-start.1 = (f32[172]{0:T(256)S(1)}, f32[172]{0:T(256)}, u32[]{:S(2)}) copy-start(f32[172]{0:T(256)} %param.19) | copy-start | bytes 2068
  100.8 26.7 %copy-start = (bf16[128,256]{1,0:T(8,128)(2,1)S(1)}, bf16[128,256]{1,0:T(8,128)(2,1)}, u32[]{:S(2)}) copy-start(bf16[128,256]{1,0:T(8,128)(2,1)} %get-tuple-element.4) | copy-start | bytes 196612

commit v18 on v13

--- a/solution.py
+++ b/solution.py
@@ -301,13 +301,15 @@
     coords_ref,
     count_ref,
     tiles_hbm,
-    gathered_ref,
+    gathered_hbm,
     out_ref,
     order_ref,
     bounds_ref,
     cursor_ref,
     tiles_ref,
     load_sem,
+    gathered_ref,
+    gathered_sem,
 ):
     chunks = load_sem.shape[0]
     size = tiles_ref.shape[0] // chunks
@@ -317,6 +319,7 @@
         )
         for c in range(chunks)
     ]
+    loads.append(pltpu.make_async_copy(gathered_hbm, gathered_ref, gathered_sem.at[0]))
     for load in loads:
         load.start()
     blocks = out_ref.shape[0]
@@ -384,7 +387,7 @@
     smem = pl.BlockSpec(memory_space=pltpu.SMEM)
     return pl.pallas_call(
         functools.partial(products_kernel, flipped, pack),
-        in_specs=[smem, smem, pl.BlockSpec(memory_space=pl.ANY), vmem],
+        in_specs=[smem, smem, pl.BlockSpec(memory_space=pl.ANY), pl.BlockSpec(memory_space=pl.ANY)],
         out_specs=vmem,
         out_shape=jax.ShapeDtypeStruct((row_blocks, *block_shape), jnp.bfloat16),
         scratch_shapes=[
@@ -393,6 +396,8 @@
             pltpu.SMEM((row_blocks,), jnp.int32),
             pltpu.VMEM(tiles.shape, tiles.dtype),
             pltpu.SemaphoreType.DMA((8,)),
+            pltpu.VMEM(gathered.shape, gathered.dtype),
+            pltpu.SemaphoreType.DMA((1,)),
         ],
     )(coords.reshape(-1), live_total.reshape(1), tiles, gathered)
 

time: 128 us -> 128 us (level)
    pallas_call x2, Pallas kernels: 18.8 us -> 11.4 us  [tile_products(): pl.pallas_call(functools.partial(products_kernel, flipped, pack), in_spec...]
    pallas_call x1, Pallas kernels: 22.3 us -> 26.8 us  [exchange(): pl.pallas_call(functools.partial(exchange_kernel, axis, other_axis, n, sp...]
    pallas_call x1, Pallas kernels: 45.6 us -> 49.3 us  [middle(): pl.pallas_call(functools.partial(middle_kernel, n_row, n_col), out_shape=...]
where the time goes in v18:
time: 128 us; the launch traced here: 127 us
  Pallas kernels  120 us (94%)
  local copies, waits for them, and re-layouts  3.61 us (3%)
  other arithmetic  2.1 us (2%)
  between operations  1.37 us (1%)
    pallas_call x1, Pallas kernels, middle(): pl.pallas_call(functools.partial(middle_kernel, n_row, n_col), out_shape=...  49.3 us
    pallas_call x1, Pallas kernels, gather(): pl.pallas_call(functools.partial(gather_kernel, n), out_shape=jax.ShapeDt...  32.7 us
    pallas_call x1, Pallas kernels, exchange(): pl.pallas_call(functools.partial(exchange_kernel, axis, other_axis, n, sp...  26.8 us
    pallas_call x2, Pallas kernels, tile_products(): pl.pallas_call(functools.partial(products_kernel, flipped, pack), in_spec...  11.4 us

profile of v18, /device:TPU:1, one launch (start us, length us, event | category | flops | bytes accessed | tf_op | source)
XLA Modules:
  0.0 127.4 jit_solution(6564015563891151223)
XLA Ops:
  0.6 0.8 copy.14
  1.4 0.7 reshape_squeeze.11.coords_ref
  2.8 32.7 %shard_map.113.gathered_hbm = bf16[32,128,128]{2,1,0:T(8,128)(2,1)} custom-call(bf16[128,128]{1,0:T(8,128)(2,1)} %bitcast.21), custom_call_target="tpu_custom_call" | custom-call | tf_op jit(solution)/shard_map/pallas_call | solution.py:143
  35.5 0.0 copy-start.2
  35.5 5.6 %shard_map.114.parts_ref = bf16[16,128,128]{2,1,0:T(8,128)(2,1)} custom-call(s32[256]{0:T(256)} %reshape_squeeze.11.coords_ref, s32[1]{0:T(128)} %bitcast.17.count_ref, bf16[128,128,128]{2,1,0:T(8,128)(2,1)} %bitcast.19, bf16[32,128,128]{2,1,0:T(8,128)(2,1)} %shard_map.113.gathered_hbm), custom_call_target="tpu_custom_call" | custom-call | tf_op jit(solution)/shard_map/pallas_call | solution.py:388
  41.1 0.0 copy-done.2
  41.1 0.7 copy.15.mask_ref
  41.8 49.3 %shard_map.115 = (bf16[128,256]{1,0:T(8,128)(2,1)}, bf16[32,172,128]{2,1,0:T(8,128)(2,1)}) custom-call(bf16[16,128,128]{2,1,0:T(8,128)(2,1)} %shard_map.114.parts_ref, bf16[128,128]{1,0:T(8,128)(2,1)} %bitcast.22, bf16[128,256]{1,0:T(8,128)(2,1)} %weight_one_ref.1, f32[1,256]{1,0:T(1,128)} %bitcast.26, s32[128,1]{1,0:T(8,128)} %copy.15.mask_ref, ...), custom_call_target="tpu_custom_call" | custom-call | tf_op jit(solution)/shard_map/pallas_call | solution.py:230
  91.2 5.9 %shard_map.116.src_ref = bf16[16,172,128]{2,1,0:T(8,128)(2,1)} custom-call(s32[256]{0:T(256)} %reshape_squeeze.11.coords_ref, s32[1]{0:T(128)} %bitcast.18.count_ref, bf16[128,128,128]{2,1,0:T(8,128)(2,1)} %bitcast.20, bf16[32,172,128]{2,1,0:T(8,128)(2,1)} %get-tuple-element.5.gathered_hbm), custom_call_target="tpu_custom_call" | custom-call | tf_op jit(solution)/shard_map/pallas_call | solution.py:388
  97.0 0.0 copy-start.1
  97.1 0.0 copy-start
  97.1 26.8 %shard_map.117 = bf16[16,172,128]{2,1,0:T(8,128)(2,1)} custom-call(bf16[16,172,128]{2,1,0:T(8,128)(2,1)} %shard_map.116.src_ref), custom_call_target="tpu_custom_call" | custom-call | tf_op jit(solution)/shard_map/pallas_call | solution.py:261
  123.9 1.2 convert_reduce_fusion
  125.1 0.0 copy-done.1
  125.1 0.9 fusion.1
  126.0 0.7 copy.16
  126.7 0.0 copy-done
  126.7 0.6 copy.19
Async XLA Ops:
  35.5 5.6 %copy-start.2 = (s32[1,1,128]{2,1,0:T(1,128)S(1)}, s32[1,1,128]{2,1,0:T(1,128)}, u32[]{:S(2)}) copy-start(s32[1,1,128]{2,1,0:T(1,128)} %param.14) | copy-start | bytes 1540
  97.0 28.1 %copy-start.1 = (f32[172]{0:T(256)S(1)}, f32[172]{0:T(256)}, u32[]{:S(2)}) copy-start(f32[172]{0:T(256)} %param.19) | copy-start | bytes 2068
  97.1 29.7 %copy-start = (bf16[128,256]{1,0:T(8,128)(2,1)S(1)}, bf16[128,256]{1,0:T(8,128)(2,1)}, u32[]{:S(2)}) copy-start(bf16[128,256]{1,0:T(8,128)(2,1)} %get-tuple-element.4) | copy-start | bytes 196612

commit v19 on v13

--- a/solution.py
+++ b/solution.py
@@ -168,6 +168,7 @@
     send_sem,
     pass_sem,
     recv_sem,
+    local_sem,
 ):
     row = lax.axis_index("row")
     me = lax.axis_index("col")
@@ -198,7 +199,9 @@
         return carry
 
     lax.fori_loop(1, n_col, send, 0)
-    landing_ref[me] = parts_ref[me]
+    own_copy = pltpu.make_async_copy(parts_ref.at[me], landing_ref.at[me], local_sem.at[0])
+    own_copy.start()
+    own_copy.wait()
 
     def finish(step, carry):
         col_copy(lax.rem(me + step, n_col), me).wait_send()
@@ -233,14 +236,15 @@
             jax.ShapeDtypeStruct(history.shape, history.dtype),
             jax.ShapeDtypeStruct((n_row, classes, nodes), jnp.bfloat16),
         ),
-        in_specs=[vmem] * 7,
+        in_specs=[pl.BlockSpec(memory_space=pl.ANY)] + [vmem] * 6,
         out_specs=(vmem, vmem),
         scratch_shapes=[
             pltpu.VMEM(parts.shape, parts.dtype),
             pltpu.SemaphoreType.DMA((n_col,)),
             pltpu.SemaphoreType.DMA((n_col,)),
         ]
-        + [pltpu.SemaphoreType.DMA((n_row,))] * 3,
+        + [pltpu.SemaphoreType.DMA((n_row,))] * 3
+        + [pltpu.SemaphoreType.DMA((1,))],
         compiler_params=pltpu.CompilerParams(collective_id=tag, has_side_effects=True),
     )(
         parts,

time: 128 us -> 128 us (level)
    pallas_call x2, Pallas kernels: 18.8 us -> 16.7 us  [tile_products(): pl.pallas_call(functools.partial(products_kernel, flipped, pack), in_spec...]
    pallas_call x1, Pallas kernels: 22.3 us -> 24 us  [exchange(): pl.pallas_call(functools.partial(exchange_kernel, axis, other_axis, n, sp...]
where the time goes in v19:
time: 128 us; the launch traced here: 127 us
  Pallas kernels  120 us (94%)
  local copies, waits for them, and re-layouts  3.61 us (3%)
  other arithmetic  2.1 us (2%)
  between operations  1.37 us (1%)
    pallas_call x1, Pallas kernels, middle(): pl.pallas_call(functools.partial(middle_kernel, n_row, n_col), out_shape=...  46.9 us
    pallas_call x1, Pallas kernels, gather(): pl.pallas_call(functools.partial(gather_kernel, n), out_shape=jax.ShapeDt...  32.7 us
    pallas_call x1, Pallas kernels, exchange(): pl.pallas_call(functools.partial(exchange_kernel, axis, other_axis, n, sp...  24 us
    pallas_call x2, Pallas kernels, tile_products(): pl.pallas_call(functools.partial(products_kernel, flipped, pack), in_spec...  16.7 us

profile of v19, /device:TPU:1, one launch (start us, length us, event | category | flops | bytes accessed | tf_op | source)
XLA Modules:
  0.0 127.3 jit_solution(4664006003682117078)
XLA Ops:
  0.6 0.8 copy.14
  1.4 0.7 reshape_squeeze.11.coords_ref
  2.8 32.7 %shard_map.113.gathered_ref = bf16[32,128,128]{2,1,0:T(8,128)(2,1)} custom-call(bf16[128,128]{1,0:T(8,128)(2,1)} %bitcast.21), custom_call_target="tpu_custom_call" | custom-call | tf_op jit(solution)/shard_map/pallas_call | solution.py:143
  35.5 0.0 copy-start.2
  35.5 7.9 %shard_map.114.parts_ref = bf16[16,128,128]{2,1,0:T(8,128)(2,1)} custom-call(s32[256]{0:T(256)} %reshape_squeeze.11.coords_ref, s32[1]{0:T(128)} %bitcast.17.count_ref, bf16[128,128,128]{2,1,0:T(8,128)(2,1)} %bitcast.19, bf16[32,128,128]{2,1,0:T(8,128)(2,1)} %shard_map.113.gathered_ref), custom_call_target="tpu_custom_call" | custom-call | tf_op jit(solution)/shard_map/pallas_call | solution.py:389
  43.4 0.0 copy-done.2
  43.4 0.7 copy.15.mask_ref
  44.2 46.9 %shard_map.115 = (bf16[128,256]{1,0:T(8,128)(2,1)}, bf16[32,172,128]{2,1,0:T(8,128)(2,1)}) custom-call(bf16[16,128,128]{2,1,0:T(8,128)(2,1)} %shard_map.114.parts_ref, bf16[128,128]{1,0:T(8,128)(2,1)} %bitcast.22, bf16[128,256]{1,0:T(8,128)(2,1)} %weight_one_ref.1, f32[1,256]{1,0:T(1,128)} %bitcast.26, s32[128,1]{1,0:T(8,128)} %copy.15.mask_ref, ...), custom_call_target="tpu_custom_call" | custom-call | tf_op jit(solution)/shard_map/pallas_call | solution.py:233
  91.1 8.8 %shard_map.116.src_ref = bf16[16,172,128]{2,1,0:T(8,128)(2,1)} custom-call(s32[256]{0:T(256)} %reshape_squeeze.11.coords_ref, s32[1]{0:T(128)} %bitcast.18.count_ref, bf16[128,128,128]{2,1,0:T(8,128)(2,1)} %bitcast.20, bf16[32,172,128]{2,1,0:T(8,128)(2,1)} %get-tuple-element.5.gathered_ref), custom_call_target="tpu_custom_call" | custom-call | tf_op jit(solution)/shard_map/pallas_call | solution.py:389
  99.9 0.0 copy-start.1
  99.9 0.0 copy-start
  99.9 24.0 %shard_map.117 = bf16[16,172,128]{2,1,0:T(8,128)(2,1)} custom-call(bf16[16,172,128]{2,1,0:T(8,128)(2,1)} %shard_map.116.src_ref), custom_call_target="tpu_custom_call" | custom-call | tf_op jit(solution)/shard_map/pallas_call | solution.py:265
  123.9 1.2 convert_reduce_fusion
  125.1 0.0 copy-done.1
  125.1 0.9 fusion.1
  126.0 0.7 copy.16
  126.7 0.0 copy-done
  126.7 0.6 copy.19
Async XLA Ops:
  35.5 8.0 %copy-start.2 = (s32[1,1,128]{2,1,0:T(1,128)S(1)}, s32[1,1,128]{2,1,0:T(1,128)}, u32[]{:S(2)}) copy-start(s32[1,1,128]{2,1,0:T(1,128)} %param.14) | copy-start | bytes 1540
  99.9 25.2 %copy-start.1 = (f32[172]{0:T(256)S(1)}, f32[172]{0:T(256)}, u32[]{:S(2)}) copy-start(f32[172]{0:T(256)} %param.19) | copy-start | bytes 2068
  99.9 26.8 %copy-start = (bf16[128,256]{1,0:T(8,128)(2,1)S(1)}, bf16[128,256]{1,0:T(8,128)(2,1)}, u32[]{:S(2)}) copy-start(bf16[128,256]{1,0:T(8,128)(2,1)} %get-tuple-element.4) | copy-start | bytes 196612
